TPU v7x, 32 devices: a whole 2x2x4 slice. The times are simulated.
32 devices in a mesh: mom: 8 (over z, core), bond: 4 (over y, x).
Axes of the slice: x: 2, y: 2, z: 4, core: 2. Of those that a mesh axis runs over, the one named last changes fastest.
Arguments:
- vertex: bfloat16 [3, 256, 512, 512], P(None, ('mom', 'bond')), may hold values from -6 to 6
- loop_matrix: bfloat16 [3, 256, 512, 512], P(None, ('mom', 'bond')), may hold values from -0.01171875 to 0.01171875
- own_mix: float32 [3, 3], replicated, may hold values from -4 to 4
- cross_mix: float32 [3, 3], replicated, may hold values from -4 to 4
- shells: int32 [512], replicated, may hold values from 0 to 4
- partner: int32 [512], replicated, may hold values from 0 to 511, as said below
- grid_index: int32 [256], replicated, may hold values from 0 to 255, each once
Outputs:
- flowed: bfloat16 [3, 256, 512, 512], P(None, ('mom', 'bond'))
Inputs may be any that keep to these rules, and one draw needn't show every extreme that they name: partner[partner[a]] = a and partner[a] != a for every bond a; partner[a] // 64 = (a // 64 + 512 // 128) % 8. `grid_index`: each grid point appears once; point k has coordinates (k // 16, k % 16).
All inputs are finite; a program needn't handle non-finite values.
Results may differ from a plain program's by a relative error of at most 0.007.
Values may be sent and summed in bfloat16 or wider, within the bound.
A program may use at most 256 MiB of HBM per device.

v0:
```python
import math

import jax
import jax.numpy as jnp
from jax import lax
from jax.sharding import PartitionSpec as P

G = 16
NB = 512
Q = 256


def cas_table(grid_index, negate):
    points = jnp.arange(Q, dtype=jnp.int32)
    disp_x = points // G
    disp_y = points % G
    wave_x = grid_index // G
    wave_y = grid_index % G
    phases = (disp_x[:, None] * wave_x[None, :] + disp_y[:, None] * wave_y[None, :]) % G
    if negate:
        phases = (G - phases) % G
    angles = phases.astype(jnp.float32) * (2.0 * math.pi / G)
    return (jnp.cos(angles) + jnp.sin(angles)).astype(jnp.bfloat16)


def cycle_index():
    points = jnp.arange(Q, dtype=jnp.int32)
    centre_x = (points // G + G // 2) % G - G // 2
    centre_y = (points % G + G // 2) % G - G // 2
    return jnp.maximum(jnp.abs(centre_x), jnp.abs(centre_y))


def per_device(vertex, loop_matrix, own_mix, cross_mix, shells, partner, grid_index):
    mom_count = lax.axis_size("mom")
    bond_count = lax.axis_size("bond")
    channels = vertex.shape[0]
    mom_local = vertex.shape[1]
    row_block = NB // mom_count
    col_block = NB // bond_count
    entries = row_block * col_block
    mom_place = lax.axis_index("mom")
    bond_place = lax.axis_index("bond")
    half_product = jnp.einsum(
        "cqab,cqbd->cqad", vertex, loop_matrix, preferred_element_type=jnp.float32
    ).astype(jnp.bfloat16)
    product = jnp.einsum(
        "cqab,cqbd->cqad", half_product, vertex, preferred_element_type=jnp.float32
    )
    rounded = product.astype(jnp.bfloat16)
    crossed_full = jnp.take(jnp.take(rounded, partner, axis=2), partner, axis=3)
    field_data = jnp.concatenate([rounded, crossed_full], axis=0)
    depth_count = field_data.shape[0]
    shaped = field_data.reshape(depth_count, mom_local, mom_count, row_block, bond_count, col_block)
    arrived_blocks = lax.all_to_all(
        lax.all_to_all(
            shaped.transpose(0, 2, 4, 1, 3, 5).reshape(
                depth_count, mom_count, bond_count, mom_local, entries
            ),
            "mom",
            split_axis=1,
            concat_axis=3,
            tiled=True,
        ),
        "bond",
        split_axis=2,
        concat_axis=3,
        tiled=True,
    )
    arrived_blocks = arrived_blocks.reshape(2 * channels, Q, entries)
    blocks = arrived_blocks[:channels]
    crossed = arrived_blocks[channels:]
    local_grid = grid_index.reshape(mom_count, bond_count, mom_local).transpose(1, 0, 2).reshape(Q)
    plus_table = cas_table(local_grid, False)
    minus_table = cas_table(local_grid, True)
    own_lattice = jnp.einsum("rq,cqe->cre", plus_table, blocks, preferred_element_type=jnp.float32)
    cross_lattice = jnp.einsum(
        "rq,cqe->cre", minus_table, crossed, preferred_element_type=jnp.float32
    )
    mixed_terms = jnp.einsum(
        "dc,cre->dre", own_mix, own_lattice, precision=lax.Precision.HIGHEST
    ) + jnp.einsum("dc,cre->dre", cross_mix, cross_lattice, precision=lax.Precision.HIGHEST)
    shell_rows = lax.dynamic_slice_in_dim(shells, mom_place * row_block, row_block)
    shell_cols = lax.dynamic_slice_in_dim(shells, bond_place * col_block, col_block)
    reach_sum = (shell_rows[:, None] + shell_cols[None, :]).reshape(entries)
    kept_mask = cycle_index()[:, None] <= reach_sum[None, :]
    projected = jnp.where(kept_mask[None], mixed_terms * (1.0 / Q), 0.0).astype(jnp.bfloat16)
    returned = jnp.einsum(
        "rq,dre->dqe", plus_table, projected, preferred_element_type=jnp.float32
    ).astype(jnp.bfloat16)
    outgoing = returned.reshape(channels, 1, 1, bond_count, mom_count * mom_local, entries)
    arrived = lax.all_to_all(
        lax.all_to_all(outgoing, "mom", split_axis=4, concat_axis=1, tiled=True),
        "bond",
        split_axis=3,
        concat_axis=2,
        tiled=True,
    )
    arrived = arrived.reshape(channels, mom_count, bond_count, mom_local, row_block, col_block)
    returned_momenta = arrived.transpose(0, 3, 1, 4, 2, 5).reshape(channels, mom_local, NB, NB)
    flowed = vertex.astype(jnp.float32) + product + returned_momenta.astype(jnp.float32)
    return flowed.astype(jnp.bfloat16)


def solution(mesh):
    in_specs = (
        P(None, ("mom", "bond"), None, None),
        P(None, ("mom", "bond"), None, None),
        P(),
        P(),
        P(),
        P(),
        P(),
    )
    out_specs = P(None, ("mom", "bond"), None, None)
    return jax.shard_map(
        per_device, mesh=mesh, in_specs=in_specs, out_specs=out_specs, check_vma=False
    )
```

profile of v0, /device:TPU:0, one launch (start us, length us, event | category | flops | bytes accessed | tf_op | source)
XLA Modules:
  0.0 1980.4 jit_solution(1450984976383078448)
XLA Ops:
  1.4 27.9 %fusion.48 = (bf16[3,8,512,512]{3,2,1,0:T(8,128)(2,1)}, f32[3,8,512,512]{3,2,1,0:T(8,128)}) fusion(bf16[3,8,512,512]{3,2,1,0:T(8,128)(2,1)} %param.7, bf16[3,8,512,512]{3,2,1,0:T(8,128)(2,1)} %param.8), kind=kOutput, calls=%fused_computation.88 | convolution fusion | flops 12897484800 | bytes 62914560 | tf_op jit(solution)/shard_map/cqab,cqbd->cqad/dot_general | solution.py:46
  29.3 14.4 copy.48
  43.7 19.2 gather_fusion
  62.9 17.1 copy.49
  86.2 30.3 %copy.50 = bf16[3,8,512,512]{2,1,3,0:T(8,128)(2,1)} copy(bf16[3,8,512,512]{2,3,1,0:T(8,128)(2,1)S(1)} %select_bitcast_fusion.1) | data formatting | bytes 25165824 | tf_op jit(solution)/shard_map/jit(_take)/select_n | solution.py:50
  116.6 19.2 gather_fusion.1
  135.7 16.7 copy.51
  152.5 10.7 select_bitcast_fusion
  163.2 17.4 pad_maximum_fusion
  180.6 35.0 %reshape.184 = bf16[6,8,8,64,4,128]{5,4,3,2,1,0:T(4,128)(2,1)} reshape(bf16[6,8,512,512]{3,2,1,0:T(8,128)(2,1)} %pad_maximum_fusion) | data formatting | bytes 50331648 | tf_op jit(solution)/shard_map/reshape | solution.py:53
  215.6 22.6 %copy.90 = bf16[6,8,8,64,4,128]{5,3,1,4,2,0:T(8,128)(2,1)} copy(bf16[6,8,8,64,4,128]{5,4,3,2,1,0:T(4,128)(2,1)} %reshape.184) | data formatting | bytes 50331648 | tf_op jit(solution)/shard_map/reshape | solution.py:53
  238.2 37.3 %reshape.185 = bf16[6,8,4,8,8192]{4,3,2,1,0:T(8,128)(2,1)} reshape(bf16[6,8,4,8,64,128]{5,4,3,2,1,0:T(8,128)(2,1)} %bitcast.72) | data formatting | bytes 50331648 | tf_op jit(solution)/shard_map/reshape | solution.py:56
  275.5 12.7 copy.53
  288.2 549.6 %all_to_all.54 = bf16[6,8,4,8,8192]{4,3,2,0,1:T(8,128)(2,1)} all-to-all(bf16[6,8,4,8,8192]{4,3,2,0,1:T(8,128)(2,1)S(1)} %copy.53), channel_id=1, replica_groups=mesh['mom'=8,'bond'=4] {'mom'}, dimensions={1} | all-to-all | bytes 50331648 | tf_op jit(solution)/shard_map/all_to_all | solution.py:55
  837.8 12.7 copy.89
  859.0 8.7 all-to-all-start.1
  870.8 268.9 %all-to-all-done.1 = bf16[6,1,4,64,8192]{4,3,0,1,2:T(8,128)(2,1)} async-done(((bf16[6,1,4,64,8192]{4,3,0,1,2:T(8,128)(2,1)}), bf16[6,1,4,64,8192]{4,3,0,1,2:T(8,128)(2,1)}, u32[]{:S(2)}, u32[]{:S(2)}) %all-to-all-start.1) | async-done | bytes 25165856 | tf_op jit(solution)/shard_map/all_to_all | solution.py:54
  1139.7 13.6 fusion.47
  1155.2 13.1 convolution_bitcast_fusion.1
  1168.3 35.9 %copy.60 = f32[3,256,8192]{2,0,1:T(4,128)} copy(f32[3,256,8192]{1,2,0:T(8,128)} %convolution_bitcast_fusion.1) | data formatting | bytes 50331648 | tf_op jit(solution)/shard_map/rq,cqe->cre/transpose | solution.py:75
  1210.6 13.2 convolution_bitcast_fusion
  1223.8 36.1 %copy.64 = f32[3,256,8192]{2,0,1:T(4,128)} copy(f32[3,256,8192]{1,2,0:T(8,128)} %convolution_bitcast_fusion) | data formatting | bytes 50331648 | tf_op jit(solution)/shard_map/rq,cqe->cre/transpose | solution.py:76
  1259.9 65.5 %fusion.24 = f32[256,8192,3]{1,2,0:T(4,128)} fusion(f32[3,256,8192]{2,0,1:T(4,128)} %copy.60, f32[3,3]{1,0:T(4,128)S(1)} %copy-done), kind=kOutput, calls=%fused_computation.49 | convolution fusion | flops 226492416 | bytes 50331684 | tf_op jit(solution)/shard_map/dc,cre->dre/dot_general | solution.py:79
  1325.4 86.9 %fusion = bf16[3,256,8192]{2,0,1:T(4,128)(2,1)} fusion(f32[256,8192,3]{1,2,0:T(4,128)} %fusion.24, pred[256,8192]{1,0:T(8,128)(4,1)S(1)} %copy-done.1, f32[3,256,8192]{2,0,1:T(4,128)} %copy.64, f32[3,3]{1,0:T(4,128)S(1)} %copy-done.2), kind=kOutput, calls=%fused_computation.7 | convolution fusion | flops 251658240 | bytes 65011748 | tf_op jit(solution)/shard_map/dc,cre->dre/dot_general | solution.py:81
  1412.3 39.1 %convolution_convert_fusion = bf16[3,8192,256]{1,2,0:T(8,128)(2,1)} fusion(bf16[3,256,8192]{2,0,1:T(4,128)(2,1)} %fusion, s32[256]{0:T(256)S(1)} %get-tuple-element.8, s32[256]{0:T(256)S(1)} %get-tuple-element.11, s32[256]{0:T(256)S(1)} %get-tuple-element.7, s32[256]{0:T(256)S(1)} %and_select_fusion.5), kind=kOutput, calls=%fused_computation.10 | convolution fusion | flops 3228696576 | bytes 25169920 | tf_op jit(solution)/shard_map/rq,dre->dqe/dot_general | solution.py:87
  1451.4 14.6 copy.66
  1466.0 276.7 %all_to_all.55 = bf16[3,1,1,4,64,8192]{5,3,0,2,1,4:T(4,128)(2,1)S(1)} all-to-all(bf16[3,1,1,4,64,8192]{5,3,0,2,1,4:T(4,128)(2,1)S(1)} %copy.66), channel_id=1, replica_groups=mesh['mom'=8,'bond'=4] {'mom'}, dimensions={4} | all-to-all | bytes 25165824 | tf_op jit(solution)/shard_map/all_to_all | solution.py:92
  1742.7 16.3 copy.91
  1759.0 141.7 %all_to_all.56 = bf16[3,8,1,4,8,8192]{5,4,1,0,2,3:T(8,128)(2,1)} all-to-all(bf16[3,8,1,4,8,8192]{5,4,1,0,2,3:T(8,128)(2,1)S(1)} %bitcast.77), channel_id=1, replica_groups=mesh['mom'=8,'bond'=4] {'bond'}, dimensions={3} | all-to-all | bytes 25165824 | tf_op jit(solution)/shard_map/all_to_all | solution.py:91
  1907.7 17.3 copy.70
  1925.0 29.5 %reshape.189 = f32[3,8,512,512]{3,2,1,0:T(8,128)} reshape(f32[3,8,8,64,4,128]{5,4,3,2,1,0:T(4,128)} %copy.70) | data formatting | bytes 50331648 | tf_op jit(solution)/shard_map/convert_element_type | solution.py:100
  1954.6 25.6 %add_convert_fusion = bf16[3,8,512,512]{3,2,1,0:T(8,128)(2,1)} fusion(f32[3,8,512,512]{3,2,1,0:T(8,128)} %reshape.189, f32[3,8,512,512]{3,2,1,0:T(8,128)} %get-tuple-element.10, bf16[3,8,512,512]{3,2,1,0:T(8,128)(2,1)} %param.7), kind=kLoop, calls=%fused_computation.6 | loop fusion | flops 25165824 | bytes 75497472 | tf_op jit(solution)/shard_map/convert_element_type | solution.py:101
  (28 shorter events, 34.4 us)
Async XLA Ops:
  0.0 1259.9 %copy-start = (f32[3,3]{1,0:T(4,128)S(1)}, f32[3,3]{1,0:T(4,128)}, u32[]{:S(2)}) copy-start(f32[3,3]{1,0:T(4,128)} %param.9) | copy-start | bytes 112
  859.0 8.8 copy-start.3
  859.0 9.0 copy-start.4
  859.0 280.7 %all-to-all-start.1 = ((bf16[6,1,4,64,8192]{4,3,0,1,2:T(8,128)(2,1)}), bf16[6,1,4,64,8192]{4,3,0,1,2:T(8,128)(2,1)}, u32[]{:S(2)}, u32[]{:S(2)}) async-start(bf16[6,1,4,64,8192]{4,3,0,1,2:T(8,128)(2,1)} %copy.55), calls=%async_computation.1 | async-start | bytes 50331648 | tf_op jit(solution)/shard_map/all_to_all | solution.py:54
  1259.9 65.5 %copy-start.1 = (pred[256,8192]{1,0:T(8,128)(4,1)S(1)}, pred[256,8192]{1,0:T(8,128)(4,1)}, u32[]{:S(2)}) copy-start(pred[256,8192]{1,0:T(8,128)(4,1)} %broadcast_compare_fusion) | copy-start | bytes 6291460
  1259.9 65.5 %copy-start.2 = (f32[3,3]{1,0:T(4,128)S(1)}, f32[3,3]{1,0:T(4,128)}, u32[]{:S(2)}) copy-start(f32[3,3]{1,0:T(4,128)} %param.10) | copy-start | bytes 112
where the time goes:
time: 1990 us; the launch traced here: 1980 us
  blocking collectives  968 us (49%)
  local copies, waits for them, and re-layouts  417 us (21%)
  waiting for transfers between devices  269 us (14%)
  matrix products  246 us (12%)
  other arithmetic  71.1 us (4%)
    all_to_all x1, blocking collectives, per_device(): lax.all_to_all(shaped.transpose(0, 2, 4, 1, 3, 5).reshape(depth_count, mo...  550 us
    all_to_all x1, blocking collectives, per_device(): lax.all_to_all(outgoing, 'mom', split_axis=4, concat_axis=1, tiled=True)  277 us
    all_to_all x1, waiting for transfers between devices, per_device(): lax.all_to_all(lax.all_to_all(shaped.transpose(0, 2, 4, 1, 3, 5).reshape(...  269 us
    all_to_all x1, blocking collectives, per_device(): lax.all_to_all(lax.all_to_all(outgoing, 'mom', split_axis=4, concat_axis=...  142 us
    dot_general x1, matrix products, per_device(): jnp.einsum('dc,cre->dre', cross_mix, cross_lattice, precision=lax.Precisi...  86.9 us
    gather x4, local copies, waits for them, and re-layouts, per_device(): crossed_full = jnp.take(jnp.take(rounded, partner, axis=2), partner, axis=3)  72.1 us
    dot_general x1, matrix products, per_device(): jnp.einsum('dc,cre->dre', own_mix, own_lattice, precision=lax.Precision.H...  65.5 us
    reshape x2, local copies, waits for them, and re-layouts, per_device(): field_data.reshape(depth_count, mom_local, mom_count, row_block, bond_cou...  57.6 us
  transfers between devices with their start and end apart: 1, of which 1 were waited for; matrix products, arithmetic and copies ran while one was open for 0% of the time, Pallas kernels for 0%

commit v1 on v0

v1 whole, which is shorter than its diff:
```python
import functools
import math

import jax
import jax.numpy as jnp
from jax import lax
from jax.experimental import pallas as pl
from jax.experimental.pallas import tpu as pltpu
from jax.sharding import PartitionSpec as P

LANES = 128
VMEM_LIMIT = 58 * 1024 * 1024
AXES = ("mom", "bond")


def cas_table(grid_index, negate):
    count = grid_index.shape[0]
    side = math.isqrt(count)
    points = jnp.arange(count, dtype=jnp.int32)
    disp_x = points // side
    disp_y = points % side
    wave_x = grid_index // side
    wave_y = grid_index % side
    phases = (disp_x[:, None] * wave_x[None, :] + disp_y[:, None] * wave_y[None, :]) % side
    if negate:
        phases = (side - phases) % side
    angles = phases.astype(jnp.float32) * (2.0 * math.pi / side)
    return (jnp.cos(angles) + jnp.sin(angles)).astype(jnp.bfloat16)


def cycle_index(count):
    side = math.isqrt(count)
    points = jnp.arange(count, dtype=jnp.int32)
    centre_x = (points // side + side // 2) % side - side // 2
    centre_y = (points % side + side // 2) % side - side // 2
    return jnp.maximum(jnp.abs(centre_x), jnp.abs(centre_y))


def dot(a, b):
    return jnp.dot(a, b, preferred_element_type=jnp.float32)


def product_kernel(mom_local, places, vertex_ref, loop_ref, pick_ref, spread_ref, base_ref, send_ref, wide_ref):
    step = pl.program_id(0)
    vertex = vertex_ref[0, 0]
    bonds = vertex.shape[0]
    half = bonds // 2
    group = half // places
    half_product = dot(vertex, loop_ref[0, 0]).astype(jnp.bfloat16)
    product = dot(half_product, vertex)
    base_ref[0] = (product + vertex.astype(jnp.float32)).astype(jnp.bfloat16)
    rounded = product.astype(jnp.bfloat16)
    left = rounded[:, :half]
    right = dot(rounded[:, half:], spread_ref[...]).astype(jnp.bfloat16)
    for side, part in enumerate((left, right)):
        upper = dot(pick_ref[...], part[half:])
        lower = part[:half].astype(jnp.float32)
        for lane in range(half // LANES):
            at = side * (half // LANES) + lane
            cols = slice(lane * LANES, (lane + 1) * LANES)
            if mom_local == 1:
                wide_ref[at, :half] = lower[:, cols]
                wide_ref[at, half:] = upper[:, cols]
            else:
                wide_ref[at, pl.ds(step, half, stride=mom_local), :] = lower[:, cols]
                wide_ref[at, pl.ds(half * mom_local + step, half, stride=mom_local), :] = upper[:, cols]

    @pl.when(step == mom_local - 1)
    def _():
        for at in range(bonds // LANES):
            cols = slice(at * LANES, (at + 1) * LANES)
            for side in range(2):
                piece = wide_ref[at, side * half * mom_local : (side + 1) * half * mom_local]
                send_ref[:, side, :, :, cols] = piece.reshape(places, group, mom_local, LANES).astype(jnp.bfloat16)


def lattice_kernel(channels, own_ref, cross_ref, plus_ref, minus_ref, back_ref, cycle_ref, reach_ref, *refs):
    received = refs[:channels]
    send_ref = refs[channels]
    places, _, _, mom_local, bonds = send_ref.shape
    count = places * mom_local
    half = bonds // 2
    blocks = [
        [
            received[c][:, side, 0].astype(jnp.float32).reshape(count, bonds).astype(jnp.bfloat16)
            for side in range(2)
        ]
        for c in range(channels)
    ]
    for side in range(2):
        mixed = None
        for c in range(channels):
            own = dot(plus_ref[...], blocks[c][side])
            crossed = dot(minus_ref[...], blocks[c][1 - side])
            crossed = jnp.concatenate([crossed[:, half:], crossed[:, :half]], axis=1)
            term = own_ref[c] * own + cross_ref[c] * crossed
            mixed = term if mixed is None else mixed + term
        kept = cycle_ref[...] <= reach_ref[side, 0]
        projected = jnp.where(kept, mixed, 0.0).astype(jnp.bfloat16)
        returned = dot(back_ref[...], projected)
        send_ref[:, side, 0] = returned.reshape(places, mom_local, bonds).astype(jnp.bfloat16)


def finish_kernel(mom_local, base_ref, received_ref, pick_ref, spread_ref, out_ref, wide_ref):
    step = pl.program_id(0)
    places, _, group, _, bonds = received_ref.shape
    half = bonds // 2

    @pl.when(step == 0)
    def _():
        for at in range(bonds // LANES):
            cols = slice(at * LANES, (at + 1) * LANES)
            for side in range(2):
                piece = received_ref[:, side, :, :, cols].astype(jnp.float32)
                wide_ref[at, side * half * mom_local : (side + 1) * half * mom_local] = piece.reshape(
                    half * mom_local, LANES
                )

    def rows_of(at):
        if mom_local == 1:
            return wide_ref[at]
        return wide_ref[at, pl.ds(step, bonds, stride=mom_local), :]

    tiles = half // LANES
    left = jnp.concatenate([rows_of(at) for at in range(tiles)], axis=1)
    right = jnp.concatenate([rows_of(at) for at in range(tiles, 2 * tiles)], axis=1)
    right = dot(right.astype(jnp.bfloat16), pick_ref[...])
    for side, part in enumerate((left, right)):
        cols = slice(side * half, (side + 1) * half)
        lower = part[:half]
        upper = dot(spread_ref[...], part[half:].astype(jnp.bfloat16))
        out_ref[0, :half, cols] = (base_ref[0, :half, cols].astype(jnp.float32) + lower).astype(jnp.bfloat16)
        out_ref[0, half:, cols] = (base_ref[0, half:, cols].astype(jnp.float32) + upper).astype(jnp.bfloat16)


def whole(shape):
    return pl.BlockSpec(shape, lambda i: (0,) * len(shape))


def params():
    return pltpu.CompilerParams(dimension_semantics=("arbitrary",), vmem_limit_bytes=VMEM_LIMIT)


def per_device(vertex, loop_matrix, own_mix, cross_mix, shells, partner, grid_index):
    places = lax.axis_size("mom") * lax.axis_size("bond")
    place = lax.axis_index("mom") * lax.axis_size("bond") + lax.axis_index("bond")
    channels, mom_local, bonds, _ = vertex.shape
    count = grid_index.shape[0]
    half = bonds // 2
    group = half // places
    tiles = bonds // LANES
    bf16 = jnp.bfloat16

    lower_partner = partner[:half] - half
    uppers = jnp.arange(half, dtype=jnp.int32)
    pick = (lower_partner[:, None] == uppers[None, :]).astype(bf16)
    spread = pick.T
    plus_table = cas_table(grid_index, False)
    minus_table = cas_table(grid_index, True)
    back_table = plus_table.T
    cycle = cycle_index(count)[:, None]
    shell_order = jnp.concatenate([shells[:half], jnp.take(shells, partner[:half])])
    shell_rows = lax.dynamic_slice_in_dim(shell_order.reshape(2, half), place * group, group, axis=1)
    reach = (shell_rows[:, :, None] + shell_order[None, None, :]).reshape(2, group, 1, bonds)
    own_scaled = own_mix * (1.0 / count)
    cross_scaled = cross_mix * (1.0 / count)

    flow_shape = (places, 2, group, mom_local, bonds)
    flow = jax.ShapeDtypeStruct(flow_shape, bf16)
    wide = pltpu.VMEM((tiles, bonds * mom_local, LANES), jnp.float32)
    square = (half, half)
    matmul = 2 * mom_local * bonds**3
    field_bytes = 2 * mom_local * bonds * bonds

    def exchange(field):
        return lax.all_to_all(field, AXES, split_axis=0, concat_axis=0, tiled=True)

    bases, arrived = [], []
    for c in range(channels):
        matrix = pl.BlockSpec((1, 1, bonds, bonds), lambda i, c=c: (c, i, 0, 0))
        base, outgoing = pl.pallas_call(
            functools.partial(product_kernel, mom_local, places),
            grid=(mom_local,),
            in_specs=[matrix, matrix, whole(square), whole(square)],
            out_specs=[pl.BlockSpec((1, bonds, bonds), lambda i: (i, 0, 0)), whole(flow_shape)],
            out_shape=[jax.ShapeDtypeStruct((mom_local, bonds, bonds), bf16), flow],
            scratch_shapes=[wide],
            compiler_params=params(),
            cost_estimate=pl.CostEstimate(flops=5 * matmul // 2, bytes_accessed=4 * field_bytes, transcendentals=0),
            name="product_%d" % c,
        )(vertex, loop_matrix, pick, spread)
        bases.append(base)
        arrived.append(exchange(outgoing))

    flow_block = pl.BlockSpec((places, 2, 1, mom_local, bonds), lambda i: (0, 0, i, 0, 0))
    table = whole((count, count))
    scalars = pl.BlockSpec(memory_space=pltpu.SMEM)
    finished = []
    for d in range(channels):
        outgoing = pl.pallas_call(
            functools.partial(lattice_kernel, channels),
            grid=(group,),
            in_specs=[
                scalars,
                scalars,
                table,
                table,
                table,
                whole((count, 1)),
                pl.BlockSpec((2, 1, 1, bonds), lambda i: (0, i, 0, 0)),
            ]
            + [flow_block] * channels,
            out_specs=flow_block,
            out_shape=flow,
            compiler_params=params(),
            cost_estimate=pl.CostEstimate(
                flops=(2 * channels + 1) * 2 * count * count * 2 * group * bonds,
                bytes_accessed=(channels + 1) * field_bytes,
                transcendentals=0,
            ),
            name="lattice_%d" % d,
        )(own_scaled[d], cross_scaled[d], plus_table, minus_table, back_table, cycle, reach, *arrived)
        finished.append(exchange(outgoing))

    results = []
    for d in range(channels):
        matrix = pl.BlockSpec((1, bonds, bonds), lambda i: (i, 0, 0))
        results.append(
            pl.pallas_call(
                functools.partial(finish_kernel, mom_local),
                grid=(mom_local,),
                in_specs=[matrix, whole(flow_shape), whole(square), whole(square)],
                out_specs=matrix,
                out_shape=jax.ShapeDtypeStruct((mom_local, bonds, bonds), bf16),
                scratch_shapes=[wide],
                compiler_params=params(),
                cost_estimate=pl.CostEstimate(flops=matmul // 2, bytes_accessed=3 * field_bytes, transcendentals=0),
                name="finish_%d" % d,
            )(bases[d], finished[d], pick, spread)
        )
    return jnp.stack(results)


def solution(mesh):
    in_specs = (P(None, AXES, None, None), P(None, AXES, None, None), P(), P(), P(), P(), P())
    return jax.shard_map(
        per_device, mesh=mesh, in_specs=in_specs, out_specs=P(None, AXES, None, None), check_vma=False
    )
```

time: 1990 us -> 657 us (0.33)
  blocking collectives: 968 us -> 0 us
  local copies, waits for them, and re-layouts: 417 us -> 2.7 us
  matrix products: 246 us -> 0 us
  waiting for transfers between devices: 269 us -> 481 us
  Pallas kernels: 0 us -> 117 us
  other arithmetic: 71.1 us -> 16.8 us
  starting transfers between devices: 8.73 us -> 37.7 us
    all_to_all x3 -> x0, blocking collectives: 968 us -> none  [the longest x1 550 us: per_device(): lax.all_to_all(shaped.transpose(0, 2, 4, 1, 3, 5).reshape(depth_count, mo...]
    dot_general x6 -> x0, matrix products: 246 us -> none  [the longest x1 86.9 us: per_device(): jnp.einsum('dc,cre->dre', cross_mix, cross_lattice, precision=lax.Precisi...]
    all_to_all x1 -> x6, waiting for transfers between devices: 269 us -> 481 us  [exchange(): return lax.all_to_all(field, AXES, split_axis=0, concat_axis=0, tiled=True)]
    reshape x7 -> x1, local copies, waits for them, and re-layouts: 122 us -> 0.01 us  [per_device(): shell_order.reshape(2, half)]
    pallas_call x0 -> x9, Pallas kernels: none -> 117 us  [the longest x3 43.8 us: per_device(): pl.pallas_call(functools.partial(lattice_kernel, channels), grid=(group,)...]
    transpose x3 -> x0, local copies, waits for them, and re-layouts: 72 us -> none  [the longest x1 36.1 us: per_device(): jnp.einsum('rq,cqe->cre', minus_table, crossed, preferred_element_type=jn...]
    gather x4 -> x1, local copies, waits for them, and re-layouts: 72.1 us -> 1.99 us  [per_device(): jnp.take(shells, partner[:half])]
    convert_element_type x3 -> x0, local copies, waits for them, and re-layouts: 61.3 us -> none  [the longest x2 46.9 us: per_device(): returned_momenta.astype(jnp.float32)]
  transfers between devices with their start and end apart: 1 -> 6, of which waited for: 1 -> 6; matrix products, arithmetic and copies ran while one was open for 0% -> 1% of each run, Pallas kernels for 0% -> 12%
where the time goes in v1:
time: 657 us; the launch traced here: 655 us
  waiting for transfers between devices  481 us (73%)
  Pallas kernels  117 us (18%)
  starting transfers between devices  37.7 us (6%)
  other arithmetic  16.8 us (3%)
    all_to_all x6, waiting for transfers between devices, exchange(): return lax.all_to_all(field, AXES, split_axis=0, concat_axis=0, tiled=True)  481 us
    pallas_call x3, Pallas kernels, per_device(): pl.pallas_call(functools.partial(lattice_kernel, channels), grid=(group,)...  43.8 us
    pallas_call x3, Pallas kernels, per_device(): pl.pallas_call(functools.partial(product_kernel, mom_local, places), grid...  41.7 us
    all_to_all x6, starting transfers between devices, exchange(): return lax.all_to_all(field, AXES, split_axis=0, concat_axis=0, tiled=True)  37.7 us
    pallas_call x3, Pallas kernels, per_device(): pl.pallas_call(functools.partial(finish_kernel, mom_local), grid=(mom_loc...  31.4 us
  transfers between devices with their start and end apart: 6, of which 6 were waited for; matrix products, arithmetic and copies ran while one was open for 1% of the time, Pallas kernels for 12%

profile of v1, /device:TPU:0, one launch (start us, length us, event | category | flops | bytes accessed | tf_op | source)
XLA Modules:
  0.0 654.8 jit_solution(13491443115351882916)
XLA Ops:
  0.0 0.7 compare_select_fusion
  0.7 2.0 gather_fusion
  2.7 0.7 and_select_fusion
  3.4 0.7 fusion.12
  4.1 13.9 %product_2.1 = (bf16[8,512,512]{2,1,0:T(8,128)(2,1)}, bf16[32,2,8,8,512]{4,3,2,1,0:T(8,128)(2,1)}) custom-call(bf16[3,8,512,512]{3,2,1,0:T(8,128)(2,1)} %vertex_ref.5, bf16[3,8,512,512]{3,2,1,0:T(8,128)(2,1)} %loop_ref.5, bf16[256,256]{1,0:T(8,128)(2,1)} %get-tuple-element.31.pick_ref, bf16[256,256]{1,0:T(8,128)(2,1)} %get-tuple-element.30.spread_ref), custom_call_target="tpu_custom_call" | custom-call | flops 5368709120 | bytes 16777216 | tf_op jit(solution)/shard_map/product_2/pallas_call | solution.py:181
  18.0 7.5 %all-to-all-start.2 = ((bf16[32,2,8,8,512]{4,3,2,1,0:T(8,128)(2,1)}), bf16[32,2,8,8,512]{4,3,2,1,0:T(8,128)(2,1)}, u32[]{:S(2)}, u32[]{:S(2)}) async-start(bf16[32,2,8,8,512]{4,3,2,1,0:T(8,128)(2,1)} %get-tuple-element.14), calls=%async_computation.2 | async-start | bytes 8388608 | tf_op jit(solution)/shard_map/all_to_all | solution.py:176
  25.5 13.9 %product_1.1 = (bf16[8,512,512]{2,1,0:T(8,128)(2,1)}, bf16[32,2,8,8,512]{4,3,2,1,0:T(8,128)(2,1)}) custom-call(bf16[3,8,512,512]{3,2,1,0:T(8,128)(2,1)} %vertex_ref.5, bf16[3,8,512,512]{3,2,1,0:T(8,128)(2,1)} %loop_ref.5, bf16[256,256]{1,0:T(8,128)(2,1)} %get-tuple-element.31.pick_ref, bf16[256,256]{1,0:T(8,128)(2,1)} %get-tuple-element.30.spread_ref), custom_call_target="tpu_custom_call" | custom-call | flops 5368709120 | bytes 16777216 | tf_op jit(solution)/shard_map/product_1/pallas_call | solution.py:181
  39.4 80.3 %all-to-all-done.2.refs_2_ = bf16[32,2,8,8,512]{4,3,2,1,0:T(8,128)(2,1)} async-done(((bf16[32,2,8,8,512]{4,3,2,1,0:T(8,128)(2,1)}), bf16[32,2,8,8,512]{4,3,2,1,0:T(8,128)(2,1)}, u32[]{:S(2)}, u32[]{:S(2)}) %all-to-all-start.2) | async-done | bytes 4194336 | tf_op jit(solution)/shard_map/all_to_all | solution.py:176
  119.7 6.0 all-to-all-start.1
  125.7 13.9 %product_0.1 = (bf16[8,512,512]{2,1,0:T(8,128)(2,1)}, bf16[32,2,8,8,512]{4,3,2,1,0:T(8,128)(2,1)}) custom-call(bf16[3,8,512,512]{3,2,1,0:T(8,128)(2,1)} %vertex_ref.5, bf16[3,8,512,512]{3,2,1,0:T(8,128)(2,1)} %loop_ref.5, bf16[256,256]{1,0:T(8,128)(2,1)} %get-tuple-element.31.pick_ref, bf16[256,256]{1,0:T(8,128)(2,1)} %get-tuple-element.30.spread_ref), custom_call_target="tpu_custom_call" | custom-call | flops 5368709120 | bytes 16777216 | tf_op jit(solution)/shard_map/product_0/pallas_call | solution.py:181
  139.6 80.2 %all-to-all-done.1.refs_1_ = bf16[32,2,8,8,512]{4,3,2,1,0:T(8,128)(2,1)} async-done(((bf16[32,2,8,8,512]{4,3,2,1,0:T(8,128)(2,1)}), bf16[32,2,8,8,512]{4,3,2,1,0:T(8,128)(2,1)}, u32[]{:S(2)}, u32[]{:S(2)}) %all-to-all-start.1) | async-done | bytes 4194336 | tf_op jit(solution)/shard_map/all_to_all | solution.py:176
  219.9 6.0 all-to-all-start
  225.9 0.1 constant_dynamic-slice_fusion
  226.0 0.8 fusion.19.cycle_ref
  226.8 0.0 copy-done.1
  226.8 0.6 slice_bitcast_fusion.4
  227.4 0.7 broadcast_add_fusion.reach_ref
  228.1 4.2 add_convert_fusion
  232.3 87.8 %all-to-all-done.refs_0_ = bf16[32,2,8,8,512]{4,3,2,1,0:T(8,128)(2,1)} async-done(((bf16[32,2,8,8,512]{4,3,2,1,0:T(8,128)(2,1)}), bf16[32,2,8,8,512]{4,3,2,1,0:T(8,128)(2,1)}, u32[]{:S(2)}, u32[]{:S(2)}) %all-to-all-start) | async-done | bytes 4194336 | tf_op jit(solution)/shard_map/all_to_all | solution.py:176
  320.1 14.6 %lattice_2.1 = bf16[32,2,8,8,512]{4,3,2,1,0:T(8,128)(2,1)} custom-call(f32[3]{0:T(128)} %get-tuple-element.34.own_ref, f32[3]{0:T(128)} %get-tuple-element.21.cross_ref, bf16[256,256]{1,0:T(8,128)(2,1)} %get-tuple-element.19.plus_ref, bf16[256,256]{1,0:T(8,128)(2,1)} %get-tuple-element.18.minus_ref, bf16[256,256]{1,0:T(8,128)(2,1)} %get-tuple-element.17.back_ref, ...), custom_call_target="tpu_custom_call" | custom-call | flops 7516192768 | bytes 16777216 | tf_op jit(solution)/shard_map/lattice_2/pallas_call | solution.py:200
  334.6 6.0 all-to-all-start.5
  340.7 14.6 %lattice_0.1 = bf16[32,2,8,8,512]{4,3,2,1,0:T(8,128)(2,1)} custom-call(f32[3]{0:T(128)} %get-tuple-element.35.own_ref, f32[3]{0:T(128)} %get-tuple-element.20.cross_ref, bf16[256,256]{1,0:T(8,128)(2,1)} %get-tuple-element.19.plus_ref, bf16[256,256]{1,0:T(8,128)(2,1)} %get-tuple-element.18.minus_ref, bf16[256,256]{1,0:T(8,128)(2,1)} %get-tuple-element.17.back_ref, ...), custom_call_target="tpu_custom_call" | custom-call | flops 7516192768 | bytes 16777216 | tf_op jit(solution)/shard_map/lattice_0/pallas_call | solution.py:200
  355.3 79.5 %all-to-all-done.5.received_ref = bf16[32,2,8,8,512]{4,3,2,1,0:T(8,128)(2,1)} async-done(((bf16[32,2,8,8,512]{4,3,2,1,0:T(8,128)(2,1)}), bf16[32,2,8,8,512]{4,3,2,1,0:T(8,128)(2,1)}, u32[]{:S(2)}, u32[]{:S(2)}) %all-to-all-start.5) | async-done | bytes 4194336 | tf_op jit(solution)/shard_map/all_to_all | solution.py:176
  434.8 6.0 all-to-all-start.3
  440.9 14.6 %lattice_1.1 = bf16[32,2,8,8,512]{4,3,2,1,0:T(8,128)(2,1)} custom-call(f32[3]{0:T(128)} %get-tuple-element.33.own_ref, f32[3]{0:T(128)} %get-tuple-element.22.cross_ref, bf16[256,256]{1,0:T(8,128)(2,1)} %get-tuple-element.19.plus_ref, bf16[256,256]{1,0:T(8,128)(2,1)} %get-tuple-element.18.minus_ref, bf16[256,256]{1,0:T(8,128)(2,1)} %get-tuple-element.17.back_ref, ...), custom_call_target="tpu_custom_call" | custom-call | flops 7516192768 | bytes 16777216 | tf_op jit(solution)/shard_map/lattice_1/pallas_call | solution.py:200
  455.5 79.6 %all-to-all-done.3.received_ref = bf16[32,2,8,8,512]{4,3,2,1,0:T(8,128)(2,1)} async-done(((bf16[32,2,8,8,512]{4,3,2,1,0:T(8,128)(2,1)}), bf16[32,2,8,8,512]{4,3,2,1,0:T(8,128)(2,1)}, u32[]{:S(2)}, u32[]{:S(2)}) %all-to-all-start.3) | async-done | bytes 4194336 | tf_op jit(solution)/shard_map/all_to_all | solution.py:176
  535.0 6.2 all-to-all-start.4
  541.2 10.4 %finish_2.1 = bf16[8,512,512]{2,1,0:T(8,128)(2,1)} custom-call(bf16[8,512,512]{2,1,0:T(8,128)(2,1)} %get-tuple-element.16.base_ref, bf16[32,2,8,8,512]{4,3,2,1,0:T(8,128)(2,1)} %all-to-all-done.5.received_ref, bf16[256,256]{1,0:T(8,128)(2,1)} %get-tuple-element.31.pick_ref, bf16[256,256]{1,0:T(8,128)(2,1)} %get-tuple-element.30.spread_ref), custom_call_target="tpu_custom_call" | custom-call | flops 1073741824 | bytes 12582912 | tf_op jit(solution)/shard_map/finish_2/pallas_call | solution.py:229
  551.7 10.3 %finish_0.1 = bf16[8,512,512]{2,1,0:T(8,128)(2,1)} custom-call(bf16[8,512,512]{2,1,0:T(8,128)(2,1)} %get-tuple-element.11.base_ref, bf16[32,2,8,8,512]{4,3,2,1,0:T(8,128)(2,1)} %all-to-all-done.3.received_ref, bf16[256,256]{1,0:T(8,128)(2,1)} %get-tuple-element.31.pick_ref, bf16[256,256]{1,0:T(8,128)(2,1)} %get-tuple-element.30.spread_ref), custom_call_target="tpu_custom_call" | custom-call | flops 1073741824 | bytes 12582912 | tf_op jit(solution)/shard_map/finish_0/pallas_call | solution.py:229
  562.0 73.2 %all-to-all-done.4.received_ref = bf16[32,2,8,8,512]{4,3,2,1,0:T(8,128)(2,1)} async-done(((bf16[32,2,8,8,512]{4,3,2,1,0:T(8,128)(2,1)}), bf16[32,2,8,8,512]{4,3,2,1,0:T(8,128)(2,1)}, u32[]{:S(2)}, u32[]{:S(2)}) %all-to-all-start.4) | async-done | bytes 4194336 | tf_op jit(solution)/shard_map/all_to_all | solution.py:176
  635.2 10.6 %finish_1.1 = bf16[8,512,512]{2,1,0:T(8,128)(2,1)} custom-call(bf16[8,512,512]{2,1,0:T(8,128)(2,1)} %get-tuple-element.15.base_ref, bf16[32,2,8,8,512]{4,3,2,1,0:T(8,128)(2,1)} %all-to-all-done.4.received_ref, bf16[256,256]{1,0:T(8,128)(2,1)} %get-tuple-element.31.pick_ref, bf16[256,256]{1,0:T(8,128)(2,1)} %get-tuple-element.30.spread_ref), custom_call_target="tpu_custom_call" | custom-call | flops 1073741824 | bytes 12582912 | tf_op jit(solution)/shard_map/finish_1/pallas_call | solution.py:229
  645.8 9.0 %pad_maximum_fusion = bf16[3,8,512,512]{3,2,1,0:T(8,128)(2,1)} fusion(bf16[1,8,512,512]{3,2,1,0:T(8,128)(2,1)S(1)} %bitcast.15, bf16[1,8,512,512]{3,2,1,0:T(8,128)(2,1)} %bitcast.17, bf16[1,8,512,512]{3,2,1,0:T(8,128)(2,1)} %bitcast.16), kind=kLoop, calls=%fused_computation.1 | loop fusion | flops 12582912 | bytes 25165824 | tf_op jit(solution)/shard_map/stack | solution.py:241
  (16 shorter events, 0.1 us)
Async XLA Ops:
  18.0 101.6 %all-to-all-start.2 = ((bf16[32,2,8,8,512]{4,3,2,1,0:T(8,128)(2,1)}), bf16[32,2,8,8,512]{4,3,2,1,0:T(8,128)(2,1)}, u32[]{:S(2)}, u32[]{:S(2)}) async-start(bf16[32,2,8,8,512]{4,3,2,1,0:T(8,128)(2,1)} %get-tuple-element.14), calls=%async_computation.2 | async-start | bytes 8388608 | tf_op jit(solution)/shard_map/all_to_all | solution.py:176
  119.7 100.2 %all-to-all-start.1 = ((bf16[32,2,8,8,512]{4,3,2,1,0:T(8,128)(2,1)}), bf16[32,2,8,8,512]{4,3,2,1,0:T(8,128)(2,1)}, u32[]{:S(2)}, u32[]{:S(2)}) async-start(bf16[32,2,8,8,512]{4,3,2,1,0:T(8,128)(2,1)} %get-tuple-element.13), calls=%async_computation.1 | async-start | bytes 8388608 | tf_op jit(solution)/shard_map/all_to_all | solution.py:176
  219.9 6.0 slice-start
  219.9 6.9 %copy-start.1 = (f32[3,3]{1,0:T(4,128)S(1)}, f32[3,3]{1,0:T(4,128)}, u32[]{:S(2)}) copy-start(f32[3,3]{1,0:T(4,128)} %param.9) | copy-start | bytes 112
  219.9 6.9 %copy-start.2 = (f32[3,3]{1,0:T(4,128)S(1)}, f32[3,3]{1,0:T(4,128)}, u32[]{:S(2)}) copy-start(f32[3,3]{1,0:T(4,128)} %param.10) | copy-start | bytes 112
  219.9 6.9 %copy-start.3 = (s32[256]{0:T(256)S(1)}, s32[256]{0:T(256)}, u32[]{:S(2)}) copy-start(s32[256]{0:T(256)} %param.13) | copy-start | bytes 3076
  219.9 100.2 %all-to-all-start = ((bf16[32,2,8,8,512]{4,3,2,1,0:T(8,128)(2,1)}), bf16[32,2,8,8,512]{4,3,2,1,0:T(8,128)(2,1)}, u32[]{:S(2)}, u32[]{:S(2)}) async-start(bf16[32,2,8,8,512]{4,3,2,1,0:T(8,128)(2,1)} %get-tuple-element.12), calls=%async_computation | async-start | bytes 8388608 | tf_op jit(solution)/shard_map/all_to_all | solution.py:176
  334.6 100.2 %all-to-all-start.5 = ((bf16[32,2,8,8,512]{4,3,2,1,0:T(8,128)(2,1)}), bf16[32,2,8,8,512]{4,3,2,1,0:T(8,128)(2,1)}, u32[]{:S(2)}, u32[]{:S(2)}) async-start(bf16[32,2,8,8,512]{4,3,2,1,0:T(8,128)(2,1)} %lattice_2.1), calls=%async_computation.5 | async-start | bytes 8388608 | tf_op jit(solution)/shard_map/all_to_all | solution.py:176
  434.8 100.2 %all-to-all-start.3 = ((bf16[32,2,8,8,512]{4,3,2,1,0:T(8,128)(2,1)}), bf16[32,2,8,8,512]{4,3,2,1,0:T(8,128)(2,1)}, u32[]{:S(2)}, u32[]{:S(2)}) async-start(bf16[32,2,8,8,512]{4,3,2,1,0:T(8,128)(2,1)} %lattice_0.1), calls=%async_computation.3 | async-start | bytes 8388608 | tf_op jit(solution)/shard_map/all_to_all | solution.py:176
  535.0 100.2 %all-to-all-start.4 = ((bf16[32,2,8,8,512]{4,3,2,1,0:T(8,128)(2,1)}), bf16[32,2,8,8,512]{4,3,2,1,0:T(8,128)(2,1)}, u32[]{:S(2)}, u32[]{:S(2)}) async-start(bf16[32,2,8,8,512]{4,3,2,1,0:T(8,128)(2,1)} %lattice_1.1), calls=%async_computation.4 | async-start | bytes 8388608 | tf_op jit(solution)/shard_map/all_to_all | solution.py:176
  635.2 10.6 %copy-start = (bf16[8,512,512]{2,1,0:T(8,128)(2,1)S(1)}, bf16[8,512,512]{2,1,0:T(8,128)(2,1)}, u32[]{:S(2)}) copy-start(bf16[8,512,512]{2,1,0:T(8,128)(2,1)} %finish_2.1) | copy-start | bytes 12582916

commit v2 on v1

v2 whole, which is shorter than its diff:
```python
import functools
import math

import jax
import jax.numpy as jnp
from jax import lax
from jax.experimental import pallas as pl
from jax.experimental.pallas import tpu as pltpu
from jax.sharding import PartitionSpec as P

LANES = 128
VMEM_LIMIT = 58 * 1024 * 1024
AXES = ("mom", "bond")


def cas_table(grid_index, negate):
    count = grid_index.shape[0]
    side = math.isqrt(count)
    points = jnp.arange(count, dtype=jnp.int32)
    disp_x = points // side
    disp_y = points % side
    wave_x = grid_index // side
    wave_y = grid_index % side
    phases = (disp_x[:, None] * wave_x[None, :] + disp_y[:, None] * wave_y[None, :]) % side
    if negate:
        phases = (side - phases) % side
    angles = phases.astype(jnp.float32) * (2.0 * math.pi / side)
    return (jnp.cos(angles) + jnp.sin(angles)).astype(jnp.bfloat16)


def cycle_index(count):
    side = math.isqrt(count)
    points = jnp.arange(count, dtype=jnp.int32)
    centre_x = (points // side + side // 2) % side - side // 2
    centre_y = (points % side + side // 2) % side - side // 2
    return jnp.maximum(jnp.abs(centre_x), jnp.abs(centre_y))


def dot(a, b):
    return jnp.dot(a, b, preferred_element_type=jnp.float32)


def product_kernel(mom_local, places, vertex_ref, loop_ref, pick_ref, spread_ref, *refs):
    base_ref, send_ref, token_ref, wide_ref = refs[-4:]
    step = pl.program_id(1)
    token_ref[...] = jnp.zeros_like(token_ref)
    vertex = vertex_ref[0, 0]
    bonds = vertex.shape[0]
    half = bonds // 2
    group = half // places
    half_product = dot(vertex, loop_ref[0, 0]).astype(jnp.bfloat16)
    product = dot(half_product, vertex)
    base_ref[0, 0] = (product + vertex.astype(jnp.float32)).astype(jnp.bfloat16)
    rounded = product.astype(jnp.bfloat16)
    left = rounded[:, :half]
    right = dot(rounded[:, half:], spread_ref[...]).astype(jnp.bfloat16)
    for side, part in enumerate((left, right)):
        upper = dot(pick_ref[...], part[half:])
        lower = part[:half].astype(jnp.float32)
        for lane in range(half // LANES):
            at = side * (half // LANES) + lane
            cols = slice(lane * LANES, (lane + 1) * LANES)
            if mom_local == 1:
                wide_ref[at, :half] = lower[:, cols]
                wide_ref[at, half:] = upper[:, cols]
            else:
                wide_ref[at, pl.ds(step, half, stride=mom_local), :] = lower[:, cols]
                wide_ref[at, pl.ds(half * mom_local + step, half, stride=mom_local), :] = upper[:, cols]

    @pl.when(step == mom_local - 1)
    def _():
        for at in range(bonds // LANES):
            cols = slice(at * LANES, (at + 1) * LANES)
            for side in range(2):
                piece = wide_ref[at, side * half * mom_local : (side + 1) * half * mom_local]
                send_ref[:, 0, side, :, :, cols] = piece.reshape(places, group, mom_local, LANES).astype(jnp.bfloat16)


def lattice_kernel(sizes, targets, own_ref, cross_ref, plus_ref, minus_ref, back_ref, cycle_ref, reach_ref, *refs):
    received = [(refs[k], n) for k, size in enumerate(sizes) for n in range(size)]
    send_ref = refs[-1]
    places, _, _, _, mom_local, bonds = send_ref.shape
    count = places * mom_local
    half = bonds // 2
    blocks = [
        [
            ref[:, n, side, 0].astype(jnp.float32).reshape(count, bonds).astype(jnp.bfloat16)
            for side in range(2)
        ]
        for ref, n in received
    ]
    for side in range(2):
        mixed = [None] * len(targets)
        for c in range(len(received)):
            own = dot(plus_ref[...], blocks[c][side])
            crossed = dot(minus_ref[...], blocks[c][1 - side])
            crossed = jnp.concatenate([crossed[:, half:], crossed[:, :half]], axis=1)
            for k, d in enumerate(targets):
                term = own_ref[d, c] * own + cross_ref[d, c] * crossed
                mixed[k] = term if c == 0 else mixed[k] + term
        kept = cycle_ref[...] <= reach_ref[side, 0]
        for k in range(len(targets)):
            projected = jnp.where(kept, mixed[k], 0.0).astype(jnp.bfloat16)
            returned = dot(back_ref[...], projected)
            send_ref[:, k, side, 0] = returned.reshape(places, mom_local, bonds).astype(jnp.bfloat16)


def finish_kernel(mom_local, base_ref, received_ref, pick_ref, spread_ref, out_ref, wide_ref):
    step = pl.program_id(1)
    places, _, _, group, _, bonds = received_ref.shape
    half = bonds // 2

    @pl.when(step == 0)
    def _():
        for at in range(bonds // LANES):
            cols = slice(at * LANES, (at + 1) * LANES)
            for side in range(2):
                piece = received_ref[:, 0, side, :, :, cols].astype(jnp.float32)
                wide_ref[at, side * half * mom_local : (side + 1) * half * mom_local] = piece.reshape(
                    half * mom_local, LANES
                )

    def rows_of(at):
        if mom_local == 1:
            return wide_ref[at]
        return wide_ref[at, pl.ds(step, bonds, stride=mom_local), :]

    tiles = half // LANES
    left = jnp.concatenate([rows_of(at) for at in range(tiles)], axis=1)
    right = jnp.concatenate([rows_of(at) for at in range(tiles, 2 * tiles)], axis=1)
    right = dot(right.astype(jnp.bfloat16), pick_ref[...])
    for side, part in enumerate((left, right)):
        cols = slice(side * half, (side + 1) * half)
        lower = part[:half]
        upper = dot(spread_ref[...], part[half:].astype(jnp.bfloat16))
        out_ref[0, 0, :half, cols] = (base_ref[0, 0, :half, cols].astype(jnp.float32) + lower).astype(jnp.bfloat16)
        out_ref[0, 0, half:, cols] = (base_ref[0, 0, half:, cols].astype(jnp.float32) + upper).astype(jnp.bfloat16)


def whole(shape):
    return pl.BlockSpec(shape, lambda *steps: (0,) * len(shape))


def params(axes):
    return pltpu.CompilerParams(dimension_semantics=("arbitrary",) * axes, vmem_limit_bytes=VMEM_LIMIT)


def per_device(vertex, loop_matrix, own_mix, cross_mix, shells, partner, grid_index):
    places = lax.axis_size("mom") * lax.axis_size("bond")
    place = lax.axis_index("mom") * lax.axis_size("bond") + lax.axis_index("bond")
    channels, mom_local, bonds, _ = vertex.shape
    count = grid_index.shape[0]
    half = bonds // 2
    group = half // places
    tiles = bonds // LANES
    bf16 = jnp.bfloat16
    first = list(range(channels))
    send_groups = [first[:1], first[1:]]
    back_groups = [first[:-1], first[-1:]]

    lower_partner = partner[:half] - half
    uppers = jnp.arange(half, dtype=jnp.int32)
    pick = (lower_partner[:, None] == uppers[None, :]).astype(bf16)
    spread = pick.T

    wide = pltpu.VMEM((tiles, bonds * mom_local, LANES), jnp.float32)
    square = (half, half)
    matmul = 2 * mom_local * bonds**3
    field_bytes = 2 * mom_local * bonds * bonds
    field = jax.ShapeDtypeStruct(vertex.shape, bf16)
    token_shape = jax.ShapeDtypeStruct((8, LANES), jnp.float32)

    def flow(members):
        return jax.ShapeDtypeStruct((places, members, 2, group, mom_local, bonds), bf16)

    def one_flow():
        return pl.BlockSpec((places, 1, 2, group, mom_local, bonds), lambda c, i: (0, c, 0, 0, 0, 0))

    def matrix_at(start):
        return pl.BlockSpec((1, 1, bonds, bonds), lambda c, i: (c + start, i, 0, 0))

    def exchange(outgoing):
        return lax.all_to_all(outgoing, AXES, split_axis=0, concat_axis=0, tiled=True)

    base, token, arrived = None, None, []
    for members in send_groups:
        matrix = matrix_at(members[0])
        size = len(members)
        carried = [] if base is None else [base]
        base, outgoing, made = pl.pallas_call(
            functools.partial(product_kernel, mom_local, places),
            grid=(size, mom_local),
            in_specs=[matrix, matrix, whole(square), whole(square)]
            + [pl.BlockSpec(memory_space=pl.ANY)] * len(carried),
            out_specs=[matrix, one_flow(), whole(token_shape.shape)],
            out_shape=[field, flow(size), token_shape],
            input_output_aliases={4: 0} if carried else {},
            scratch_shapes=[wide],
            compiler_params=params(2),
            cost_estimate=pl.CostEstimate(
                flops=5 * size * matmul // 2, bytes_accessed=4 * size * field_bytes, transcendentals=0
            ),
            name="product_%d" % members[0],
        )(vertex, loop_matrix, pick, spread, *carried)
        token = made if token is None else token
        arrived.append(exchange(outgoing))

    shells, partner, grid_index, own_mix, cross_mix, _ = lax.optimization_barrier(
        (shells, partner, grid_index, own_mix, cross_mix, token)
    )
    plus_table = cas_table(grid_index, False)
    minus_table = cas_table(grid_index, True)
    back_table = plus_table.T
    cycle = cycle_index(count)[:, None]
    shell_order = jnp.concatenate([shells[:half], jnp.take(shells, partner[:half])])
    shell_rows = lax.dynamic_slice_in_dim(shell_order.reshape(2, half), place * group, group, axis=1)
    reach = (shell_rows[:, :, None] + shell_order[None, None, :]).reshape(2, group, 1, bonds)
    own_scaled = own_mix * (1.0 / count)
    cross_scaled = cross_mix * (1.0 / count)

    def row_block(members):
        return pl.BlockSpec((places, members, 2, 1, mom_local, bonds), lambda i: (0, 0, 0, i, 0, 0))

    table = whole((count, count))
    scalars = pl.BlockSpec(memory_space=pltpu.SMEM)
    sizes = [len(members) for members in send_groups]
    finished, earlier = [], []
    for members in back_groups:
        size = len(members)
        outgoing = pl.pallas_call(
            functools.partial(lattice_kernel, sizes, members),
            grid=(group,),
            in_specs=[
                scalars,
                scalars,
                table,
                table,
                table,
                whole((count, 1)),
                pl.BlockSpec((2, 1, 1, bonds), lambda i: (0, i, 0, 0)),
            ]
            + [row_block(n) for n in sizes]
            + [pl.BlockSpec(memory_space=pl.ANY)] * len(earlier),
            out_specs=row_block(size),
            out_shape=flow(size),
            compiler_params=params(1),
            cost_estimate=pl.CostEstimate(
                flops=(2 * channels + size) * 2 * count * count * 2 * group * bonds,
                bytes_accessed=(channels + size) * field_bytes,
                transcendentals=0,
            ),
            name="lattice_%d" % members[0],
        )(own_scaled, cross_scaled, plus_table, minus_table, back_table, cycle, reach, *arrived, *earlier)
        earlier = [outgoing]
        finished.append(exchange(outgoing))

    for members, received in zip(back_groups, finished):
        matrix = matrix_at(members[0])
        size = len(members)
        base = pl.pallas_call(
            functools.partial(finish_kernel, mom_local),
            grid=(size, mom_local),
            in_specs=[matrix, one_flow(), whole(square), whole(square)],
            out_specs=matrix,
            out_shape=field,
            input_output_aliases={0: 0},
            scratch_shapes=[wide],
            compiler_params=params(2),
            cost_estimate=pl.CostEstimate(
                flops=size * matmul // 2, bytes_accessed=3 * size * field_bytes, transcendentals=0
            ),
            name="finish_%d" % members[0],
        )(base, received, pick, spread)
    return base


def solution(mesh):
    in_specs = (P(None, AXES, None, None), P(None, AXES, None, None), P(), P(), P(), P(), P())
    return jax.shard_map(
        per_device, mesh=mesh, in_specs=in_specs, out_specs=P(None, AXES, None, None), check_vma=False
    )
```

time: 657 us -> 636 us (0.968)
  waiting for transfers between devices: 481 us -> 497 us
  Pallas kernels: 117 us -> 103 us
  starting transfers between devices: 37.7 us -> 24.6 us
  other arithmetic: 16.8 us -> 7.65 us
    all_to_all x6 -> x4, waiting for transfers between devices: 481 us -> 497 us  [exchange(): lax.all_to_all(outgoing, AXES, split_axis=0, concat_axis=0, tiled=True)]
    all_to_all x6 -> x4, starting transfers between devices: 37.7 us -> 24.6 us  [exchange(): lax.all_to_all(outgoing, AXES, split_axis=0, concat_axis=0, tiled=True)]
    pallas_call x6 -> x4, Pallas kernels: 75.2 us -> 63.5 us  [the longest x2 33.5 us: per_device(): pl.pallas_call(functools.partial(lattice_kernel, sizes, members), grid=(g...]
    another operation x1 -> x0, other arithmetic: 8.99 us -> none  [per_device(): return jnp.stack(results)]
    pallas_call x3 -> x2, Pallas kernels: 41.7 us -> 39.2 us  [per_device(): pl.pallas_call(functools.partial(product_kernel, mom_local, places), grid...]
  transfers between devices with their start and end apart: 6 -> 4, of which waited for: 6 -> 4; matrix products, arithmetic and copies ran while one was open for 1% -> 1% of each run, Pallas kernels for 12% -> 9%
where the time goes in v2:
time: 636 us; the launch traced here: 635 us
  waiting for transfers between devices  497 us (78%)
  Pallas kernels  103 us (16%)
  starting transfers between devices  24.6 us (4%)
  other arithmetic  7.65 us (1%)
    all_to_all x4, waiting for transfers between devices, exchange(): lax.all_to_all(outgoing, AXES, split_axis=0, concat_axis=0, tiled=True)  497 us
    pallas_call x2, Pallas kernels, per_device(): pl.pallas_call(functools.partial(product_kernel, mom_local, places), grid...  39.2 us
    pallas_call x2, Pallas kernels, per_device(): pl.pallas_call(functools.partial(lattice_kernel, sizes, members), grid=(g...  33.5 us
    pallas_call x2, Pallas kernels, per_device(): pl.pallas_call(functools.partial(finish_kernel, mom_local), grid=(size, m...  30 us
    all_to_all x4, starting transfers between devices, exchange(): lax.all_to_all(outgoing, AXES, split_axis=0, concat_axis=0, tiled=True)  24.6 us
  transfers between devices with their start and end apart: 4, of which 4 were waited for; matrix products, arithmetic and copies ran while one was open for 1% of the time, Pallas kernels for 9%

profile of v2, /device:TPU:0, one launch (start us, length us, event | category | flops | bytes accessed | tf_op | source)
XLA Modules:
  0.0 634.7 jit_solution(15035355166876628445)
XLA Ops:
  0.0 0.7 slice_add_fusion
  0.7 0.8 fusion.12
  1.4 13.9 %product_0.1 = (bf16[3,8,512,512]{3,2,1,0:T(8,128)(2,1)}, bf16[32,1,2,8,8,512]{5,4,3,2,1,0:T(8,128)(2,1)}, f32[8,128]{1,0:T(8,128)}) custom-call(bf16[3,8,512,512]{3,2,1,0:T(8,128)(2,1)} %vertex_ref.3, bf16[3,8,512,512]{3,2,1,0:T(8,128)(2,1)} %loop_ref.3, bf16[256,256]{1,0:T(8,128)(2,1)} %get-tuple-element.29.pick_ref, ...), custom_call_target="tpu_custom_call" | custom-call | flops 5368709120 | bytes 16777216 | tf_op jit(solution)/shard_map/product_0/pallas_call | solution.py:190
  15.3 7.5 %all-to-all-start = ((bf16[32,1,2,8,8,512]{5,4,3,2,1,0:T(8,128)(2,1)}), bf16[32,1,2,8,8,512]{5,4,3,2,1,0:T(8,128)(2,1)}, u32[]{:S(2)}, u32[]{:S(2)}) async-start(bf16[32,1,2,8,8,512]{5,4,3,2,1,0:T(8,128)(2,1)} %get-tuple-element.21), calls=%async_computation | async-start | bytes 8388608 | tf_op jit(solution)/shard_map/all_to_all | solution.py:183
  22.8 25.3 %product_1.1 = (bf16[3,8,512,512]{3,2,1,0:T(8,128)(2,1)}, bf16[32,2,2,8,8,512]{5,4,3,2,1,0:T(8,128)(2,1)}, f32[8,128]{1,0:T(8,128)}) custom-call(bf16[3,8,512,512]{3,2,1,0:T(8,128)(2,1)} %vertex_ref.3, bf16[3,8,512,512]{3,2,1,0:T(8,128)(2,1)} %loop_ref.3, bf16[256,256]{1,0:T(8,128)(2,1)} %get-tuple-element.29.pick_ref, ...), custom_call_target="tpu_custom_call", output_to_operand_aliasing={{0}: (4, {})} | custom-call | flops 10737418240 | bytes 33554432 | tf_op jit(solution)/shard_map/product_1/pallas_call | solution.py:190
  48.1 68.8 %all-to-all-done.refs_0_ = bf16[32,1,2,8,8,512]{5,4,3,2,1,0:T(8,128)(2,1)} async-done(((bf16[32,1,2,8,8,512]{5,4,3,2,1,0:T(8,128)(2,1)}), bf16[32,1,2,8,8,512]{5,4,3,2,1,0:T(8,128)(2,1)}, u32[]{:S(2)}, u32[]{:S(2)}) %all-to-all-start) | async-done | bytes 4194336 | tf_op jit(solution)/shard_map/all_to_all | solution.py:183
  117.0 0.0 copy-start.1
  117.0 0.0 copy-start.4
  117.0 0.0 copy-start.2
  117.0 0.0 copy-start.3
  117.0 6.0 all-to-all-start.1
  123.0 0.0 copy-done.1
  123.0 0.0 copy-done.4
  123.1 0.0 copy-done
  123.1 1.9 gather_fusion
  125.1 0.0 slice-done
  125.1 0.1 constant_dynamic-slice_fusion
  125.2 0.8 fusion.19.cycle_ref
  126.0 0.0 copy-done.2
  126.0 0.0 copy-done.3
  126.0 0.5 broadcast_multiply_fusion
  126.5 0.7 broadcast_add_fusion.reach_ref
  127.2 4.2 add_convert_fusion
  131.4 180.2 %all-to-all-done.1.refs_1_ = bf16[32,2,2,8,8,512]{5,4,3,2,1,0:T(8,128)(2,1)} async-done(((bf16[32,2,2,8,8,512]{5,4,3,2,1,0:T(8,128)(2,1)}), bf16[32,2,2,8,8,512]{5,4,3,2,1,0:T(8,128)(2,1)}, u32[]{:S(2)}, u32[]{:S(2)}) %all-to-all-start.1) | async-done | bytes 8388640 | tf_op jit(solution)/shard_map/all_to_all | solution.py:183
  311.5 18.9 %lattice_0.1.refs_2_ = bf16[32,2,2,8,8,512]{5,4,3,2,1,0:T(8,128)(2,1)} custom-call(f32[3,3]{1,0:T(4,128)} %get-tuple-element.32.own_ref, f32[3,3]{1,0:T(4,128)} %get-tuple-element.31.cross_ref, bf16[256,256]{1,0:T(8,128)(2,1)} %get-tuple-element.25.plus_ref, bf16[256,256]{1,0:T(8,128)(2,1)} %get-tuple-element.24.minus_ref, ...), custom_call_target="tpu_custom_call" | custom-call | flops 8589934592 | bytes 20971520 | tf_op jit(solution)/shard_map/lattice_0/pallas_call | solution.py:230
  330.4 5.6 all-to-all-start.2
  336.0 14.7 %lattice_2.1 = bf16[32,1,2,8,8,512]{5,4,3,2,1,0:T(8,128)(2,1)} custom-call(f32[3,3]{1,0:T(4,128)} %get-tuple-element.32.own_ref, f32[3,3]{1,0:T(4,128)} %get-tuple-element.31.cross_ref, bf16[256,256]{1,0:T(8,128)(2,1)} %get-tuple-element.25.plus_ref, bf16[256,256]{1,0:T(8,128)(2,1)} %get-tuple-element.24.minus_ref, ...), custom_call_target="tpu_custom_call" | custom-call | flops 7516192768 | bytes 16777216 | tf_op jit(solution)/shard_map/lattice_2/pallas_call | solution.py:230
  350.7 173.9 %all-to-all-done.2.received_ref = bf16[32,2,2,8,8,512]{5,4,3,2,1,0:T(8,128)(2,1)} async-done(((bf16[32,2,2,8,8,512]{5,4,3,2,1,0:T(8,128)(2,1)}), bf16[32,2,2,8,8,512]{5,4,3,2,1,0:T(8,128)(2,1)}, u32[]{:S(2)}, u32[]{:S(2)}) %all-to-all-start.2) | async-done | bytes 8388640 | tf_op jit(solution)/shard_map/all_to_all | solution.py:183
  524.5 5.6 all-to-all-start.3
  530.1 19.6 %finish_0.1.base_ref = bf16[3,8,512,512]{3,2,1,0:T(8,128)(2,1)} custom-call(bf16[3,8,512,512]{3,2,1,0:T(8,128)(2,1)} %get-tuple-element.15.base_ref, bf16[32,2,2,8,8,512]{5,4,3,2,1,0:T(8,128)(2,1)} %all-to-all-done.2.received_ref, bf16[256,256]{1,0:T(8,128)(2,1)} %get-tuple-element.29.pick_ref, ...), custom_call_target="tpu_custom_call", output_to_operand_aliasing={{}: (0, {})} | custom-call | flops 2147483648 | bytes 25165824 | tf_op jit(solution)/shard_map/finish_0/pallas_call | solution.py:260
  549.7 74.6 %all-to-all-done.3.received_ref = bf16[32,1,2,8,8,512]{5,4,3,2,1,0:T(8,128)(2,1)} async-done(((bf16[32,1,2,8,8,512]{5,4,3,2,1,0:T(8,128)(2,1)}), bf16[32,1,2,8,8,512]{5,4,3,2,1,0:T(8,128)(2,1)}, u32[]{:S(2)}, u32[]{:S(2)}) %all-to-all-start.3) | async-done | bytes 4194336 | tf_op jit(solution)/shard_map/all_to_all | solution.py:183
  624.3 10.4 %finish_2.1 = bf16[3,8,512,512]{3,2,1,0:T(8,128)(2,1)} custom-call(bf16[3,8,512,512]{3,2,1,0:T(8,128)(2,1)} %finish_0.1.base_ref, bf16[32,1,2,8,8,512]{5,4,3,2,1,0:T(8,128)(2,1)} %all-to-all-done.3.received_ref, bf16[256,256]{1,0:T(8,128)(2,1)} %get-tuple-element.29.pick_ref, ...), custom_call_target="tpu_custom_call", output_to_operand_aliasing={{}: (0, {})} | custom-call | flops 1073741824 | bytes 12582912 | tf_op jit(solution)/shard_map/finish_2/pallas_call | solution.py:260
  (8 shorter events, 0.1 us)
Async XLA Ops:
  15.3 101.6 %all-to-all-start = ((bf16[32,1,2,8,8,512]{5,4,3,2,1,0:T(8,128)(2,1)}), bf16[32,1,2,8,8,512]{5,4,3,2,1,0:T(8,128)(2,1)}, u32[]{:S(2)}, u32[]{:S(2)}) async-start(bf16[32,1,2,8,8,512]{5,4,3,2,1,0:T(8,128)(2,1)} %get-tuple-element.21), calls=%async_computation | async-start | bytes 8388608 | tf_op jit(solution)/shard_map/all_to_all | solution.py:183
  117.0 6.1 copy-start.1
  117.0 6.1 copy-start.4
  117.0 6.1 copy-start
  117.0 8.1 %slice-start = ((s32[512]{0:T(512)}), s32[256]{0:T(256)S(1)}, s32[]{:S(2)}) async-start(s32[512]{0:T(512)} %param.11), calls=%async_computation.4 | async-start | bytes 2048 | tf_op jit(solution)/shard_map/slice | solution.py:215
  117.0 9.0 %copy-start.2 = (f32[3,3]{1,0:T(4,128)S(1)}, f32[3,3]{1,0:T(4,128)}, u32[]{:S(2)}) copy-start(f32[3,3]{1,0:T(4,128)} %param.10) | copy-start | bytes 112
  117.0 9.0 %copy-start.3 = (f32[3,3]{1,0:T(4,128)S(1)}, f32[3,3]{1,0:T(4,128)}, u32[]{:S(2)}) copy-start(f32[3,3]{1,0:T(4,128)} %param.9) | copy-start | bytes 112
  117.0 194.5 %all-to-all-start.1 = ((bf16[32,2,2,8,8,512]{5,4,3,2,1,0:T(8,128)(2,1)}), bf16[32,2,2,8,8,512]{5,4,3,2,1,0:T(8,128)(2,1)}, u32[]{:S(2)}, u32[]{:S(2)}) async-start(bf16[32,2,2,8,8,512]{5,4,3,2,1,0:T(8,128)(2,1)} %get-tuple-element.22), calls=%async_computation.1 | async-start | bytes 16777216 | tf_op jit(solution)/shard_map/all_to_all | solution.py:183
  330.4 194.1 %all-to-all-start.2 = ((bf16[32,2,2,8,8,512]{5,4,3,2,1,0:T(8,128)(2,1)}), bf16[32,2,2,8,8,512]{5,4,3,2,1,0:T(8,128)(2,1)}, u32[]{:S(2)}, u32[]{:S(2)}) async-start(bf16[32,2,2,8,8,512]{5,4,3,2,1,0:T(8,128)(2,1)} %lattice_0.1.refs_2_), calls=%async_computation.2 | async-start | bytes 16777216 | tf_op jit(solution)/shard_map/all_to_all | solution.py:183
  524.5 99.8 %all-to-all-start.3 = ((bf16[32,1,2,8,8,512]{5,4,3,2,1,0:T(8,128)(2,1)}), bf16[32,1,2,8,8,512]{5,4,3,2,1,0:T(8,128)(2,1)}, u32[]{:S(2)}, u32[]{:S(2)}) async-start(bf16[32,1,2,8,8,512]{5,4,3,2,1,0:T(8,128)(2,1)} %lattice_2.1), calls=%async_computation.3 | async-start | bytes 8388608 | tf_op jit(solution)/shard_map/all_to_all | solution.py:183

commit v3 on v2

--- a/solution.py
+++ b/solution.py
@@ -5,10 +5,12 @@
 import jax.numpy as jnp
 from jax import lax
 from jax.experimental import pallas as pl
+from jax.experimental.layout import Layout, with_layout_constraint
 from jax.experimental.pallas import tpu as pltpu
 from jax.sharding import PartitionSpec as P
 
 LANES = 128
+PAIR = 2
 VMEM_LIMIT = 58 * 1024 * 1024
 AXES = ("mom", "bond")
 
@@ -74,6 +76,27 @@
             for side in range(2):
                 piece = wide_ref[at, side * half * mom_local : (side + 1) * half * mom_local]
                 send_ref[:, 0, side, :, :, cols] = piece.reshape(places, group, mom_local, LANES).astype(jnp.bfloat16)
+
+
+def first_product_kernel(places, vertex_ref, loop_ref, pick_ref, spread_ref, base_ref, send_ref, token_ref):
+    token_ref[...] = jnp.zeros_like(token_ref)
+    bonds = vertex_ref.shape[-1]
+    half = bonds // 2
+    group = half // places
+    for n in range(vertex_ref.shape[1]):
+        vertex = vertex_ref[0, n]
+        half_product = dot(vertex, loop_ref[0, n]).astype(jnp.bfloat16)
+        product = dot(half_product, vertex)
+        base_ref[0, n] = (product + vertex.astype(jnp.float32)).astype(jnp.bfloat16)
+        rounded = product.astype(jnp.bfloat16)
+        left = rounded[:, :half]
+        right = dot(rounded[:, half:], spread_ref[...]).astype(jnp.bfloat16)
+        for side, part in enumerate((left, right)):
+            cols = slice(side * half, (side + 1) * half)
+            lower = part[:half].astype(jnp.float32)
+            upper = dot(pick_ref[...], part[half:])
+            send_ref[:, 0, n, 0, :, cols] = lower.reshape(places, group, half).astype(jnp.bfloat16)
+            send_ref[:, 0, n, 1, :, cols] = upper.reshape(places, group, half).astype(jnp.bfloat16)
 
 
 def lattice_kernel(sizes, targets, own_ref, cross_ref, plus_ref, minus_ref, back_ref, cycle_ref, reach_ref, *refs):
@@ -137,6 +160,22 @@
         out_ref[0, 0, half:, cols] = (base_ref[0, 0, half:, cols].astype(jnp.float32) + upper).astype(jnp.bfloat16)
 
 
+def last_finish_kernel(base_ref, received_ref, pick_ref, spread_ref, out_ref):
+    bonds = base_ref.shape[-1]
+    half = bonds // 2
+    for n in range(base_ref.shape[1]):
+        for side in range(2):
+            cols = slice(side * half, (side + 1) * half)
+            lower = received_ref[:, 0, n, 0, :, cols].astype(jnp.float32).reshape(half, half)
+            upper = received_ref[:, 0, n, 1, :, cols].astype(jnp.float32).reshape(half, half).astype(jnp.bfloat16)
+            if side:
+                lower = dot(lower.astype(jnp.bfloat16), pick_ref[...])
+                upper = dot(upper, pick_ref[...]).astype(jnp.bfloat16)
+            upper = dot(spread_ref[...], upper)
+            out_ref[0, n, :half, cols] = (base_ref[0, n, :half, cols].astype(jnp.float32) + lower).astype(jnp.bfloat16)
+            out_ref[0, n, half:, cols] = (base_ref[0, n, half:, cols].astype(jnp.float32) + upper).astype(jnp.bfloat16)
+
+
 def whole(shape):
     return pl.BlockSpec(shape, lambda *steps: (0,) * len(shape))
 
@@ -182,27 +221,43 @@
     def exchange(outgoing):
         return lax.all_to_all(outgoing, AXES, split_axis=0, concat_axis=0, tiled=True)
 
-    base, token, arrived = None, None, []
-    for members in send_groups:
+    pair = PAIR if mom_local % PAIR == 0 else 1
+    plain = jax.ShapeDtypeStruct((places, 1, mom_local, 2, group, bonds), bf16)
+    plain_block = pl.BlockSpec((places, 1, pair, 2, group, bonds), lambda i: (0, 0, i, 0, 0, 0))
+
+    def pair_at(start):
+        return pl.BlockSpec((1, pair, bonds, bonds), lambda i: (start, i, 0, 0))
+
+    base, outgoing, token = pl.pallas_call(
+        functools.partial(first_product_kernel, places),
+        grid=(mom_local // pair,),
+        in_specs=[pair_at(0), pair_at(0), whole(square), whole(square)],
+        out_specs=[pair_at(0), plain_block, whole(token_shape.shape)],
+        out_shape=[field, plain, token_shape],
+        compiler_params=params(1),
+        cost_estimate=pl.CostEstimate(flops=5 * matmul // 2, bytes_accessed=4 * field_bytes, transcendentals=0),
+        name="product_first",
+    )(vertex, loop_matrix, pick, spread)
+    whole_rows = with_layout_constraint(exchange(outgoing), Layout(major_to_minor=tuple(range(6))))
+    arrived = [whole_rows.transpose(0, 1, 3, 4, 2, 5)]
+    for members in send_groups[1:]:
         matrix = matrix_at(members[0])
         size = len(members)
-        carried = [] if base is None else [base]
-        base, outgoing, made = pl.pallas_call(
+        base, outgoing, _ = pl.pallas_call(
             functools.partial(product_kernel, mom_local, places),
             grid=(size, mom_local),
             in_specs=[matrix, matrix, whole(square), whole(square)]
-            + [pl.BlockSpec(memory_space=pl.ANY)] * len(carried),
+            + [pl.BlockSpec(memory_space=pl.ANY)],
             out_specs=[matrix, one_flow(), whole(token_shape.shape)],
             out_shape=[field, flow(size), token_shape],
-            input_output_aliases={4: 0} if carried else {},
+            input_output_aliases={4: 0},
             scratch_shapes=[wide],
             compiler_params=params(2),
             cost_estimate=pl.CostEstimate(
                 flops=5 * size * matmul // 2, bytes_accessed=4 * size * field_bytes, transcendentals=0
             ),
             name="product_%d" % members[0],
-        )(vertex, loop_matrix, pick, spread, *carried)
-        token = made if token is None else token
+        )(vertex, loop_matrix, pick, spread, base)
         arrived.append(exchange(outgoing))
 
     shells, partner, grid_index, own_mix, cross_mix, _ = lax.optimization_barrier(
@@ -252,9 +307,11 @@
             name="lattice_%d" % members[0],
         )(own_scaled, cross_scaled, plus_table, minus_table, back_table, cycle, reach, *arrived, *earlier)
         earlier = [outgoing]
+        if members is back_groups[-1]:
+            outgoing = outgoing.transpose(0, 1, 4, 2, 3, 5)
         finished.append(exchange(outgoing))
 
-    for members, received in zip(back_groups, finished):
+    for members, received in zip(back_groups[:-1], finished[:-1]):
         matrix = matrix_at(members[0])
         size = len(members)
         base = pl.pallas_call(
@@ -271,7 +328,18 @@
             ),
             name="finish_%d" % members[0],
         )(base, received, pick, spread)
-    return base
+    last = back_groups[-1][0]
+    return pl.pallas_call(
+        last_finish_kernel,
+        grid=(mom_local // pair,),
+        in_specs=[pair_at(last), plain_block, whole(square), whole(square)],
+        out_specs=pair_at(last),
+        out_shape=field,
+        input_output_aliases={0: 0},
+        compiler_params=params(1),
+        cost_estimate=pl.CostEstimate(flops=matmul // 2, bytes_accessed=3 * field_bytes, transcendentals=0),
+        name="finish_last",
+    )(base, finished[-1], pick, spread)
 
 
 def solution(mesh):

time: 636 us -> 629 us (0.989)
  waiting for transfers between devices: 497 us -> 482 us
  local copies, waits for them, and re-layouts: 2.06 us -> 17 us
  Pallas kernels: 103 us -> 95.7 us
    pallas_call x0 -> x2, Pallas kernels: none -> 17.2 us  [the longest x1 10.3 us: per_device(): pl.pallas_call(functools.partial(first_product_kernel, places), grid=(mom...]
    all_to_all x4, waiting for transfers between devices: 497 us -> 482 us  [exchange(): lax.all_to_all(outgoing, AXES, split_axis=0, concat_axis=0, tiled=True)]
    pallas_call x2 -> x1, Pallas kernels: 39.2 us -> 25.3 us  [per_device(): pl.pallas_call(functools.partial(product_kernel, mom_local, places), grid...]
    pallas_call x2 -> x1, Pallas kernels: 30 us -> 19.6 us  [per_device(): pl.pallas_call(functools.partial(finish_kernel, mom_local), grid=(size, m...]
    another operation x0 -> x1, local copies, waits for them, and re-layouts: none -> 8.92 us  [per_device(): with_layout_constraint(exchange(outgoing), Layout(major_to_minor=tuple(ra...]
  transfers between devices with their start and end apart: 4 -> 4, of which waited for: 4 -> 4; matrix products, arithmetic and copies ran while one was open for 1% -> 4% of each run, Pallas kernels for 9% -> 9%
where the time goes in v3:
time: 629 us; the launch traced here: 628 us
  waiting for transfers between devices  482 us (77%)
  Pallas kernels  95.7 us (15%)
  starting transfers between devices  25.1 us (4%)
  local copies, waits for them, and re-layouts  17 us (3%)
  other arithmetic  7.65 us (1%)
    all_to_all x4, waiting for transfers between devices, exchange(): lax.all_to_all(outgoing, AXES, split_axis=0, concat_axis=0, tiled=True)  482 us
    pallas_call x2, Pallas kernels, per_device(): pl.pallas_call(functools.partial(lattice_kernel, sizes, members), grid=(g...  33.5 us
    pallas_call x1, Pallas kernels, per_device(): pl.pallas_call(functools.partial(product_kernel, mom_local, places), grid...  25.3 us
    all_to_all x4, starting transfers between devices, exchange(): lax.all_to_all(outgoing, AXES, split_axis=0, concat_axis=0, tiled=True)  25.1 us
    pallas_call x1, Pallas kernels, per_device(): pl.pallas_call(functools.partial(finish_kernel, mom_local), grid=(size, m...  19.6 us
  transfers between devices with their start and end apart: 4, of which 4 were waited for; matrix products, arithmetic and copies ran while one was open for 4% of the time, Pallas kernels for 9%

profile of v3, /device:TPU:0, one launch (start us, length us, event | category | flops | bytes accessed | tf_op | source)
XLA Modules:
  0.0 627.6 jit_solution(10853780527812151020)
XLA Ops:
  0.0 0.7 slice_add_fusion
  0.7 0.8 fusion.12
  1.4 10.3 %product_first.1 = (bf16[3,8,512,512]{3,2,1,0:T(8,128)(2,1)}, bf16[32,1,8,2,8,512]{5,4,3,2,1,0:T(8,128)(2,1)}, f32[8,128]{1,0:T(8,128)}) custom-call(bf16[3,8,512,512]{3,2,1,0:T(8,128)(2,1)} %vertex_ref.3, bf16[3,8,512,512]{3,2,1,0:T(8,128)(2,1)} %loop_ref.3, bf16[256,256]{1,0:T(8,128)(2,1)} %get-tuple-element.29.pick_ref, ...), custom_call_target="tpu_custom_call" | custom-call | flops 5368709120 | bytes 16777216 | tf_op jit(solution)/shard_map/product_first/pallas_call | solution.py:231
  11.8 7.5 %all-to-all-start = ((bf16[32,1,8,2,8,512]{5,4,3,2,1,0:T(8,128)(2,1)}), bf16[32,1,8,2,8,512]{5,4,3,2,1,0:T(8,128)(2,1)}, u32[]{:S(2)}, u32[]{:S(2)}) async-start(bf16[32,1,8,2,8,512]{5,4,3,2,1,0:T(8,128)(2,1)} %get-tuple-element.21), calls=%async_computation | async-start | bytes 8388608 | tf_op jit(solution)/shard_map/all_to_all | solution.py:222
  19.2 25.3 %product_1.1 = (bf16[3,8,512,512]{3,2,1,0:T(8,128)(2,1)}, bf16[32,2,2,8,8,512]{5,4,3,2,1,0:T(8,128)(2,1)}, f32[8,128]{1,0:T(8,128)}) custom-call(bf16[3,8,512,512]{3,2,1,0:T(8,128)(2,1)} %vertex_ref.3, bf16[3,8,512,512]{3,2,1,0:T(8,128)(2,1)} %loop_ref.3, bf16[256,256]{1,0:T(8,128)(2,1)} %get-tuple-element.29.pick_ref, ...), custom_call_target="tpu_custom_call", output_to_operand_aliasing={{0}: (4, {})} | custom-call | flops 10737418240 | bytes 33554432 | tf_op jit(solution)/shard_map/product_1/pallas_call | solution.py:246
  44.6 68.8 %all-to-all-done = bf16[32,1,8,2,8,512]{5,4,3,2,1,0:T(8,128)(2,1)} async-done(((bf16[32,1,8,2,8,512]{5,4,3,2,1,0:T(8,128)(2,1)}), bf16[32,1,8,2,8,512]{5,4,3,2,1,0:T(8,128)(2,1)}, u32[]{:S(2)}, u32[]{:S(2)}) %all-to-all-start) | async-done | bytes 4194336 | tf_op jit(solution)/shard_map/all_to_all | solution.py:222
  113.4 0.0 copy-start.2
  113.4 0.0 copy-start.3
  113.4 6.2 all-to-all-start.1
  119.6 0.0 copy-done.1
  119.6 0.0 copy-done.4
  119.7 0.0 copy-done
  119.7 1.9 gather_fusion
  121.7 0.0 slice-done
  121.7 0.1 constant_dynamic-slice_fusion
  121.8 0.8 fusion.19.cycle_ref
  122.6 0.0 copy-done.2
  122.6 0.0 copy-done.3
  122.6 0.5 broadcast_multiply_fusion
  123.1 0.7 broadcast_add_fusion.reach_ref
  123.8 4.2 add_convert_fusion
  128.0 8.9 %copy.22 = bf16[32,1,8,2,8,512]{5,2,4,3,1,0:T(8,128)(2,1)} copy(bf16[32,1,8,2,8,512]{5,4,3,2,1,0:T(8,128)(2,1)} %all-to-all-done) | data formatting | bytes 8388608 | tf_op jit(solution)/shard_map/layout_constraint | solution.py:241
  136.9 170.8 %all-to-all-done.1.refs_1_ = bf16[32,2,2,8,8,512]{5,4,3,2,1,0:T(8,128)(2,1)} async-done(((bf16[32,2,2,8,8,512]{5,4,3,2,1,0:T(8,128)(2,1)}), bf16[32,2,2,8,8,512]{5,4,3,2,1,0:T(8,128)(2,1)}, u32[]{:S(2)}, u32[]{:S(2)}) %all-to-all-start.1) | async-done | bytes 8388640 | tf_op jit(solution)/shard_map/all_to_all | solution.py:222
  307.7 18.9 %lattice_0.1.refs_2_ = bf16[32,2,2,8,8,512]{5,4,3,2,1,0:T(8,128)(2,1)} custom-call(f32[3,3]{1,0:T(4,128)} %get-tuple-element.32.own_ref, f32[3,3]{1,0:T(4,128)} %get-tuple-element.31.cross_ref, bf16[256,256]{1,0:T(8,128)(2,1)} %get-tuple-element.25.plus_ref, bf16[256,256]{1,0:T(8,128)(2,1)} %get-tuple-element.24.minus_ref, ...), custom_call_target="tpu_custom_call" | custom-call | flops 8589934592 | bytes 20971520 | tf_op jit(solution)/shard_map/lattice_0/pallas_call | solution.py:285
  326.5 5.9 all-to-all-start.2
  332.4 14.7 %lattice_2.1 = bf16[32,1,2,8,8,512]{5,4,3,2,1,0:T(8,128)(2,1)} custom-call(f32[3,3]{1,0:T(4,128)} %get-tuple-element.32.own_ref, f32[3,3]{1,0:T(4,128)} %get-tuple-element.31.cross_ref, bf16[256,256]{1,0:T(8,128)(2,1)} %get-tuple-element.25.plus_ref, bf16[256,256]{1,0:T(8,128)(2,1)} %get-tuple-element.24.minus_ref, ...), custom_call_target="tpu_custom_call" | custom-call | flops 7516192768 | bytes 16777216 | tf_op jit(solution)/shard_map/lattice_2/pallas_call | solution.py:285
  347.1 6.0 copy.21
  353.1 167.9 %all-to-all-done.2.received_ref = bf16[32,2,2,8,8,512]{5,4,3,2,1,0:T(8,128)(2,1)} async-done(((bf16[32,2,2,8,8,512]{5,4,3,2,1,0:T(8,128)(2,1)}), bf16[32,2,2,8,8,512]{5,4,3,2,1,0:T(8,128)(2,1)}, u32[]{:S(2)}, u32[]{:S(2)}) %all-to-all-start.2) | async-done | bytes 8388640 | tf_op jit(solution)/shard_map/all_to_all | solution.py:222
  520.9 5.6 all-to-all-start.3
  526.5 19.6 %finish_0.1.base_ref = bf16[3,8,512,512]{3,2,1,0:T(8,128)(2,1)} custom-call(bf16[3,8,512,512]{3,2,1,0:T(8,128)(2,1)} %get-tuple-element.15.base_ref, bf16[32,2,2,8,8,512]{5,4,3,2,1,0:T(8,128)(2,1)} %all-to-all-done.2.received_ref, bf16[256,256]{1,0:T(8,128)(2,1)} %get-tuple-element.29.pick_ref, ...), custom_call_target="tpu_custom_call", output_to_operand_aliasing={{}: (0, {})} | custom-call | flops 2147483648 | bytes 25165824 | tf_op jit(solution)/shard_map/finish_0/pallas_call | solution.py:317
  546.1 74.6 %all-to-all-done.3.received_ref = bf16[32,1,8,2,8,512]{5,4,3,2,1,0:T(8,128)(2,1)} async-done(((bf16[32,1,8,2,8,512]{5,4,3,2,1,0:T(8,128)(2,1)}), bf16[32,1,8,2,8,512]{5,4,3,2,1,0:T(8,128)(2,1)}, u32[]{:S(2)}, u32[]{:S(2)}) %all-to-all-start.3) | async-done | bytes 4194336 | tf_op jit(solution)/shard_map/all_to_all | solution.py:222
  620.7 6.9 %finish_last.1 = bf16[3,8,512,512]{3,2,1,0:T(8,128)(2,1)} custom-call(bf16[3,8,512,512]{3,2,1,0:T(8,128)(2,1)} %finish_0.1.base_ref, bf16[32,1,8,2,8,512]{5,4,3,2,1,0:T(8,128)(2,1)} %all-to-all-done.3.received_ref, bf16[256,256]{1,0:T(8,128)(2,1)} %get-tuple-element.29.pick_ref, ...), custom_call_target="tpu_custom_call", output_to_operand_aliasing={{}: (0, {})} | custom-call | flops 1073741824 | bytes 12582912 | tf_op jit(solution)/shard_map/finish_last/pallas_call | solution.py:332
  (10 shorter events, 0.1 us)
Async XLA Ops:
  11.8 101.6 %all-to-all-start = ((bf16[32,1,8,2,8,512]{5,4,3,2,1,0:T(8,128)(2,1)}), bf16[32,1,8,2,8,512]{5,4,3,2,1,0:T(8,128)(2,1)}, u32[]{:S(2)}, u32[]{:S(2)}) async-start(bf16[32,1,8,2,8,512]{5,4,3,2,1,0:T(8,128)(2,1)} %get-tuple-element.21), calls=%async_computation | async-start | bytes 8388608 | tf_op jit(solution)/shard_map/all_to_all | solution.py:222
  113.4 6.2 copy-start.1
  113.4 6.3 copy-start.4
  113.4 6.3 %copy-start = (s32[512]{0:T(512)S(1)}, s32[512]{0:T(512)}, u32[]{:S(2)}) copy-start(s32[512]{0:T(512)} %param.11) | copy-start | bytes 6148
  113.4 8.3 %slice-start = ((s32[512]{0:T(512)}), s32[256]{0:T(256)S(1)}, s32[]{:S(2)}) async-start(s32[512]{0:T(512)} %param.11), calls=%async_computation.4 | async-start | bytes 2048 | tf_op jit(solution)/shard_map/slice | solution.py:270
  113.4 9.2 %copy-start.2 = (f32[3,3]{1,0:T(4,128)S(1)}, f32[3,3]{1,0:T(4,128)}, u32[]{:S(2)}) copy-start(f32[3,3]{1,0:T(4,128)} %param.10) | copy-start | bytes 112
  113.4 9.2 %copy-start.3 = (f32[3,3]{1,0:T(4,128)S(1)}, f32[3,3]{1,0:T(4,128)}, u32[]{:S(2)}) copy-start(f32[3,3]{1,0:T(4,128)} %param.9) | copy-start | bytes 112
  113.4 194.2 %all-to-all-start.1 = ((bf16[32,2,2,8,8,512]{5,4,3,2,1,0:T(8,128)(2,1)}), bf16[32,2,2,8,8,512]{5,4,3,2,1,0:T(8,128)(2,1)}, u32[]{:S(2)}, u32[]{:S(2)}) async-start(bf16[32,2,2,8,8,512]{5,4,3,2,1,0:T(8,128)(2,1)} %get-tuple-element.22), calls=%async_computation.1 | async-start | bytes 16777216 | tf_op jit(solution)/shard_map/all_to_all | solution.py:222
  326.5 194.4 %all-to-all-start.2 = ((bf16[32,2,2,8,8,512]{5,4,3,2,1,0:T(8,128)(2,1)}), bf16[32,2,2,8,8,512]{5,4,3,2,1,0:T(8,128)(2,1)}, u32[]{:S(2)}, u32[]{:S(2)}) async-start(bf16[32,2,2,8,8,512]{5,4,3,2,1,0:T(8,128)(2,1)} %lattice_0.1.refs_2_), calls=%async_computation.2 | async-start | bytes 16777216 | tf_op jit(solution)/shard_map/all_to_all | solution.py:222
  520.9 99.8 %all-to-all-start.3 = ((bf16[32,1,8,2,8,512]{5,4,3,2,1,0:T(8,128)(2,1)}), bf16[32,1,8,2,8,512]{5,4,3,2,1,0:T(8,128)(2,1)}, u32[]{:S(2)}, u32[]{:S(2)}) async-start(bf16[32,1,8,2,8,512]{5,4,3,2,1,0:T(8,128)(2,1)} %bitcast.6), calls=%async_computation.3 | async-start | bytes 8388608 | tf_op jit(solution)/shard_map/all_to_all | solution.py:222

commit v4 on v3

--- a/solution.py
+++ b/solution.py
@@ -11,6 +11,7 @@
 
 LANES = 128
 PAIR = 2
+ROWS = 2
 VMEM_LIMIT = 58 * 1024 * 1024
 AXES = ("mom", "bond")
 
@@ -105,27 +106,28 @@
     places, _, _, _, mom_local, bonds = send_ref.shape
     count = places * mom_local
     half = bonds // 2
-    blocks = [
-        [
-            ref[:, n, side, 0].astype(jnp.float32).reshape(count, bonds).astype(jnp.bfloat16)
-            for side in range(2)
+    for row in range(send_ref.shape[3]):
+        blocks = [
+            [
+                ref[:, n, side, row].astype(jnp.float32).reshape(count, bonds).astype(jnp.bfloat16)
+                for side in range(2)
+            ]
+            for ref, n in received
         ]
-        for ref, n in received
-    ]
-    for side in range(2):
-        mixed = [None] * len(targets)
-        for c in range(len(received)):
-            own = dot(plus_ref[...], blocks[c][side])
-            crossed = dot(minus_ref[...], blocks[c][1 - side])
-            crossed = jnp.concatenate([crossed[:, half:], crossed[:, :half]], axis=1)
-            for k, d in enumerate(targets):
-                term = own_ref[d, c] * own + cross_ref[d, c] * crossed
-                mixed[k] = term if c == 0 else mixed[k] + term
-        kept = cycle_ref[...] <= reach_ref[side, 0]
-        for k in range(len(targets)):
-            projected = jnp.where(kept, mixed[k], 0.0).astype(jnp.bfloat16)
-            returned = dot(back_ref[...], projected)
-            send_ref[:, k, side, 0] = returned.reshape(places, mom_local, bonds).astype(jnp.bfloat16)
+        for side in range(2):
+            mixed = [None] * len(targets)
+            for c in range(len(received)):
+                own = dot(plus_ref[...], blocks[c][side])
+                crossed = dot(minus_ref[...], blocks[c][1 - side])
+                crossed = jnp.concatenate([crossed[:, half:], crossed[:, :half]], axis=1)
+                for k, d in enumerate(targets):
+                    term = own_ref[d, c] * own + cross_ref[d, c] * crossed
+                    mixed[k] = term if c == 0 else mixed[k] + term
+            kept = cycle_ref[...] <= reach_ref[side, row]
+            for k in range(len(targets)):
+                projected = jnp.where(kept, mixed[k], 0.0).astype(jnp.bfloat16)
+                returned = dot(back_ref[...], projected)
+                send_ref[:, k, side, row] = returned.reshape(places, mom_local, bonds).astype(jnp.bfloat16)
 
 
 def finish_kernel(mom_local, base_ref, received_ref, pick_ref, spread_ref, out_ref, wide_ref):
@@ -273,8 +275,10 @@
     own_scaled = own_mix * (1.0 / count)
     cross_scaled = cross_mix * (1.0 / count)
 
+    rows = ROWS if group % ROWS == 0 else 1
+
     def row_block(members):
-        return pl.BlockSpec((places, members, 2, 1, mom_local, bonds), lambda i: (0, 0, 0, i, 0, 0))
+        return pl.BlockSpec((places, members, 2, rows, mom_local, bonds), lambda i: (0, 0, 0, i, 0, 0))
 
     table = whole((count, count))
     scalars = pl.BlockSpec(memory_space=pltpu.SMEM)
@@ -284,7 +288,7 @@
         size = len(members)
         outgoing = pl.pallas_call(
             functools.partial(lattice_kernel, sizes, members),
-            grid=(group,),
+            grid=(group // rows,),
             in_specs=[
                 scalars,
                 scalars,
@@ -292,7 +296,7 @@
                 table,
                 table,
                 whole((count, 1)),
-                pl.BlockSpec((2, 1, 1, bonds), lambda i: (0, i, 0, 0)),
+                pl.BlockSpec((2, rows, 1, bonds), lambda i: (0, i, 0, 0)),
             ]
             + [row_block(n) for n in sizes]
             + [pl.BlockSpec(memory_space=pl.ANY)] * len(earlier),

time: 629 us -> 629 us (level)
  no operation moved by 1% of the time
where the time goes in v4:
time: 629 us; the launch traced here: 628 us
  waiting for transfers between devices  482 us (77%)
  Pallas kernels  95.1 us (15%)
  starting transfers between devices  25.8 us (4%)
  local copies, waits for them, and re-layouts  17 us (3%)
  other arithmetic  7.65 us (1%)
    all_to_all x4, waiting for transfers between devices, exchange(): lax.all_to_all(outgoing, AXES, split_axis=0, concat_axis=0, tiled=True)  482 us
    pallas_call x2, Pallas kernels, per_device(): pl.pallas_call(functools.partial(lattice_kernel, sizes, members), grid=(g...  33 us
    all_to_all x4, starting transfers between devices, exchange(): lax.all_to_all(outgoing, AXES, split_axis=0, concat_axis=0, tiled=True)  25.8 us
    pallas_call x1, Pallas kernels, per_device(): pl.pallas_call(functools.partial(product_kernel, mom_local, places), grid...  25.3 us
    pallas_call x1, Pallas kernels, per_device(): pl.pallas_call(functools.partial(finish_kernel, mom_local), grid=(size, m...  19.6 us
  transfers between devices with their start and end apart: 4, of which 4 were waited for; matrix products, arithmetic and copies ran while one was open for 4% of the time, Pallas kernels for 9%

profile of v4, /device:TPU:0, one launch (start us, length us, event | category | flops | bytes accessed | tf_op | source)
XLA Modules:
  0.0 627.6 jit_solution(10003250402630697154)
XLA Ops:
  0.0 0.7 slice_add_fusion
  0.7 0.8 fusion.12
  1.4 10.3 %product_first.1 = (bf16[3,8,512,512]{3,2,1,0:T(8,128)(2,1)}, bf16[32,1,8,2,8,512]{5,4,3,2,1,0:T(8,128)(2,1)}, f32[8,128]{1,0:T(8,128)}) custom-call(bf16[3,8,512,512]{3,2,1,0:T(8,128)(2,1)} %vertex_ref.3, bf16[3,8,512,512]{3,2,1,0:T(8,128)(2,1)} %loop_ref.3, bf16[256,256]{1,0:T(8,128)(2,1)} %get-tuple-element.29.pick_ref, ...), custom_call_target="tpu_custom_call" | custom-call | flops 5368709120 | bytes 16777216 | tf_op jit(solution)/shard_map/product_first/pallas_call | solution.py:233
  11.8 7.5 %all-to-all-start = ((bf16[32,1,8,2,8,512]{5,4,3,2,1,0:T(8,128)(2,1)}), bf16[32,1,8,2,8,512]{5,4,3,2,1,0:T(8,128)(2,1)}, u32[]{:S(2)}, u32[]{:S(2)}) async-start(bf16[32,1,8,2,8,512]{5,4,3,2,1,0:T(8,128)(2,1)} %get-tuple-element.21), calls=%async_computation | async-start | bytes 8388608 | tf_op jit(solution)/shard_map/all_to_all | solution.py:224
  19.2 25.3 %product_1.1 = (bf16[3,8,512,512]{3,2,1,0:T(8,128)(2,1)}, bf16[32,2,2,8,8,512]{5,4,3,2,1,0:T(8,128)(2,1)}, f32[8,128]{1,0:T(8,128)}) custom-call(bf16[3,8,512,512]{3,2,1,0:T(8,128)(2,1)} %vertex_ref.3, bf16[3,8,512,512]{3,2,1,0:T(8,128)(2,1)} %loop_ref.3, bf16[256,256]{1,0:T(8,128)(2,1)} %get-tuple-element.29.pick_ref, ...), custom_call_target="tpu_custom_call", output_to_operand_aliasing={{0}: (4, {})} | custom-call | flops 10737418240 | bytes 33554432 | tf_op jit(solution)/shard_map/product_1/pallas_call | solution.py:248
  44.6 68.8 %all-to-all-done = bf16[32,1,8,2,8,512]{5,4,3,2,1,0:T(8,128)(2,1)} async-done(((bf16[32,1,8,2,8,512]{5,4,3,2,1,0:T(8,128)(2,1)}), bf16[32,1,8,2,8,512]{5,4,3,2,1,0:T(8,128)(2,1)}, u32[]{:S(2)}, u32[]{:S(2)}) %all-to-all-start) | async-done | bytes 4194336 | tf_op jit(solution)/shard_map/all_to_all | solution.py:224
  113.4 0.0 copy-start.2
  113.4 0.0 copy-start.3
  113.4 6.2 all-to-all-start.1
  119.6 0.0 copy-done.1
  119.6 0.0 copy-done.4
  119.7 0.0 copy-done
  119.7 1.9 gather_fusion
  121.7 0.0 slice-done
  121.7 0.1 constant_dynamic-slice_fusion
  121.8 0.8 fusion.19.cycle_ref
  122.6 0.0 copy-done.2
  122.6 0.0 copy-done.3
  122.6 0.5 broadcast_multiply_fusion
  123.1 0.7 broadcast_add_fusion.reach_ref
  123.8 4.2 add_convert_fusion
  128.0 8.9 %copy.22 = bf16[32,1,8,2,8,512]{5,2,4,3,1,0:T(8,128)(2,1)} copy(bf16[32,1,8,2,8,512]{5,4,3,2,1,0:T(8,128)(2,1)} %all-to-all-done) | data formatting | bytes 8388608 | tf_op jit(solution)/shard_map/layout_constraint | solution.py:243
  136.9 170.8 %all-to-all-done.1.refs_1_ = bf16[32,2,2,8,8,512]{5,4,3,2,1,0:T(8,128)(2,1)} async-done(((bf16[32,2,2,8,8,512]{5,4,3,2,1,0:T(8,128)(2,1)}), bf16[32,2,2,8,8,512]{5,4,3,2,1,0:T(8,128)(2,1)}, u32[]{:S(2)}, u32[]{:S(2)}) %all-to-all-start.1) | async-done | bytes 8388640 | tf_op jit(solution)/shard_map/all_to_all | solution.py:224
  307.7 18.8 %lattice_0.1.refs_2_ = bf16[32,2,2,8,8,512]{5,4,3,2,1,0:T(8,128)(2,1)} custom-call(f32[3,3]{1,0:T(4,128)} %get-tuple-element.32.own_ref, f32[3,3]{1,0:T(4,128)} %get-tuple-element.31.cross_ref, bf16[256,256]{1,0:T(8,128)(2,1)} %get-tuple-element.25.plus_ref, bf16[256,256]{1,0:T(8,128)(2,1)} %get-tuple-element.24.minus_ref, ...), custom_call_target="tpu_custom_call" | custom-call | flops 8589934592 | bytes 20971520 | tf_op jit(solution)/shard_map/lattice_0/pallas_call | solution.py:289
  326.5 6.1 all-to-all-start.2
  332.6 14.1 %lattice_2.1 = bf16[32,1,2,8,8,512]{5,4,3,2,1,0:T(8,128)(2,1)} custom-call(f32[3,3]{1,0:T(4,128)} %get-tuple-element.32.own_ref, f32[3,3]{1,0:T(4,128)} %get-tuple-element.31.cross_ref, bf16[256,256]{1,0:T(8,128)(2,1)} %get-tuple-element.25.plus_ref, bf16[256,256]{1,0:T(8,128)(2,1)} %get-tuple-element.24.minus_ref, ...), custom_call_target="tpu_custom_call" | custom-call | flops 7516192768 | bytes 16777216 | tf_op jit(solution)/shard_map/lattice_2/pallas_call | solution.py:289
  346.8 6.0 copy.21
  352.7 167.8 %all-to-all-done.2.received_ref = bf16[32,2,2,8,8,512]{5,4,3,2,1,0:T(8,128)(2,1)} async-done(((bf16[32,2,2,8,8,512]{5,4,3,2,1,0:T(8,128)(2,1)}), bf16[32,2,2,8,8,512]{5,4,3,2,1,0:T(8,128)(2,1)}, u32[]{:S(2)}, u32[]{:S(2)}) %all-to-all-start.2) | async-done | bytes 8388640 | tf_op jit(solution)/shard_map/all_to_all | solution.py:224
  520.5 6.0 all-to-all-start.3
  526.5 19.6 %finish_0.1.base_ref = bf16[3,8,512,512]{3,2,1,0:T(8,128)(2,1)} custom-call(bf16[3,8,512,512]{3,2,1,0:T(8,128)(2,1)} %get-tuple-element.15.base_ref, bf16[32,2,2,8,8,512]{5,4,3,2,1,0:T(8,128)(2,1)} %all-to-all-done.2.received_ref, bf16[256,256]{1,0:T(8,128)(2,1)} %get-tuple-element.29.pick_ref, ...), custom_call_target="tpu_custom_call", output_to_operand_aliasing={{}: (0, {})} | custom-call | flops 2147483648 | bytes 25165824 | tf_op jit(solution)/shard_map/finish_0/pallas_call | solution.py:321
  546.1 74.6 %all-to-all-done.3.received_ref = bf16[32,1,8,2,8,512]{5,4,3,2,1,0:T(8,128)(2,1)} async-done(((bf16[32,1,8,2,8,512]{5,4,3,2,1,0:T(8,128)(2,1)}), bf16[32,1,8,2,8,512]{5,4,3,2,1,0:T(8,128)(2,1)}, u32[]{:S(2)}, u32[]{:S(2)}) %all-to-all-start.3) | async-done | bytes 4194336 | tf_op jit(solution)/shard_map/all_to_all | solution.py:224
  620.7 6.9 %finish_last.1 = bf16[3,8,512,512]{3,2,1,0:T(8,128)(2,1)} custom-call(bf16[3,8,512,512]{3,2,1,0:T(8,128)(2,1)} %finish_0.1.base_ref, bf16[32,1,8,2,8,512]{5,4,3,2,1,0:T(8,128)(2,1)} %all-to-all-done.3.received_ref, bf16[256,256]{1,0:T(8,128)(2,1)} %get-tuple-element.29.pick_ref, ...), custom_call_target="tpu_custom_call", output_to_operand_aliasing={{}: (0, {})} | custom-call | flops 1073741824 | bytes 12582912 | tf_op jit(solution)/shard_map/finish_last/pallas_call | solution.py:336
  (10 shorter events, 0.1 us)
Async XLA Ops:
  11.8 101.6 %all-to-all-start = ((bf16[32,1,8,2,8,512]{5,4,3,2,1,0:T(8,128)(2,1)}), bf16[32,1,8,2,8,512]{5,4,3,2,1,0:T(8,128)(2,1)}, u32[]{:S(2)}, u32[]{:S(2)}) async-start(bf16[32,1,8,2,8,512]{5,4,3,2,1,0:T(8,128)(2,1)} %get-tuple-element.21), calls=%async_computation | async-start | bytes 8388608 | tf_op jit(solution)/shard_map/all_to_all | solution.py:224
  113.4 6.2 copy-start.1
  113.4 6.3 copy-start.4
  113.4 6.3 %copy-start = (s32[512]{0:T(512)S(1)}, s32[512]{0:T(512)}, u32[]{:S(2)}) copy-start(s32[512]{0:T(512)} %param.11) | copy-start | bytes 6148
  113.4 8.3 %slice-start = ((s32[512]{0:T(512)}), s32[256]{0:T(256)S(1)}, s32[]{:S(2)}) async-start(s32[512]{0:T(512)} %param.11), calls=%async_computation.4 | async-start | bytes 2048 | tf_op jit(solution)/shard_map/slice | solution.py:272
  113.4 9.2 %copy-start.2 = (f32[3,3]{1,0:T(4,128)S(1)}, f32[3,3]{1,0:T(4,128)}, u32[]{:S(2)}) copy-start(f32[3,3]{1,0:T(4,128)} %param.10) | copy-start | bytes 112
  113.4 9.2 %copy-start.3 = (f32[3,3]{1,0:T(4,128)S(1)}, f32[3,3]{1,0:T(4,128)}, u32[]{:S(2)}) copy-start(f32[3,3]{1,0:T(4,128)} %param.9) | copy-start | bytes 112
  113.4 194.2 %all-to-all-start.1 = ((bf16[32,2,2,8,8,512]{5,4,3,2,1,0:T(8,128)(2,1)}), bf16[32,2,2,8,8,512]{5,4,3,2,1,0:T(8,128)(2,1)}, u32[]{:S(2)}, u32[]{:S(2)}) async-start(bf16[32,2,2,8,8,512]{5,4,3,2,1,0:T(8,128)(2,1)} %get-tuple-element.22), calls=%async_computation.1 | async-start | bytes 16777216 | tf_op jit(solution)/shard_map/all_to_all | solution.py:224
  326.5 194.0 %all-to-all-start.2 = ((bf16[32,2,2,8,8,512]{5,4,3,2,1,0:T(8,128)(2,1)}), bf16[32,2,2,8,8,512]{5,4,3,2,1,0:T(8,128)(2,1)}, u32[]{:S(2)}, u32[]{:S(2)}) async-start(bf16[32,2,2,8,8,512]{5,4,3,2,1,0:T(8,128)(2,1)} %lattice_0.1.refs_2_), calls=%async_computation.2 | async-start | bytes 16777216 | tf_op jit(solution)/shard_map/all_to_all | solution.py:224
  520.5 100.2 %all-to-all-start.3 = ((bf16[32,1,8,2,8,512]{5,4,3,2,1,0:T(8,128)(2,1)}), bf16[32,1,8,2,8,512]{5,4,3,2,1,0:T(8,128)(2,1)}, u32[]{:S(2)}, u32[]{:S(2)}) async-start(bf16[32,1,8,2,8,512]{5,4,3,2,1,0:T(8,128)(2,1)} %bitcast.6), calls=%async_computation.3 | async-start | bytes 8388608 | tf_op jit(solution)/shard_map/all_to_all | solution.py:224
